TPU v7x, 32 devices: a whole 2x2x4 slice. The times are simulated.
32 devices in a mesh: stn: 4 (over y, x), chan: 4 (over z), beam: 2 (over core).
Axes of the slice: x: 2, y: 2, z: 4, core: 2. Of those that a mesh axis runs over, the one named last changes fastest.
Arguments:
- volts: bfloat16 [2, 128, 12, 9216], P(None, 'stn', 'chan', 'beam'), may hold values from -6 to 6
- taps: float32 [16, 256], replicated, may hold values from -1.5 to 1.5
- delays: int32 [32, 128], P(None, 'stn'), may hold values from 0 to 1023
- station_sub: int32 [128], P('stn'), may hold values from 0 to 3
- beam_sub: int32 [32], replicated, may hold values from 0 to 3
Outputs:
- beams: float32 [32, 2, 12, 48, 256], P(('stn', 'chan', 'beam'))
All inputs are finite; a program needn't handle non-finite values.
Results may differ from a plain program's by a relative error of at most 0.014.
Values may be sent and summed in bfloat16 or wider, within the bound.
A program may use at most 192 MiB of HBM per device.

v0:
```python
import functools
import math

import jax
import jax.numpy as jnp
import numpy as np
from jax import lax
from jax.experimental import pallas as pl
from jax.experimental.pallas import tpu as pltpu
from jax.sharding import PartitionSpec as P

SUBARRAYS = 4
UNROLL = 4
LANES = 128
VMEM_LIMIT = 32 * 2**20
MESH = pl.DeviceIdType.MESH


def dft_tables(fine):
    index = np.arange(fine)
    angle = 2.0 * np.pi * (index[:, None] * index[None, :] % fine) / fine
    scale = 1.0 / math.sqrt(fine)
    return (
        jnp.asarray(np.cos(angle) * scale, jnp.bfloat16),
        jnp.asarray(np.sin(angle) * scale, jnp.bfloat16),
    )


def unit_turn(turn):
    quarter = (turn + 8192) >> 14
    t = (turn - (quarter << 14)).astype(jnp.float32) * (2.0 * math.pi / 65536.0)
    u = t * t
    sine = t * (1.0 + u * (-1.0 / 6 + u * (1.0 / 120 + u * (-1.0 / 5040))))
    cosine = 1.0 + u * (-0.5 + u * (1.0 / 24 + u * (-1.0 / 720 + u * (1.0 / 40320))))
    odd = (quarter & 1) == 1
    c = jnp.where(odd, sine, cosine)
    s = jnp.where(odd, cosine, sine)
    c = jnp.where(((quarter + 1) & 2) == 2, -c, c)
    s = jnp.where((quarter & 2) == 2, -s, s)
    return c, s


def beam_kernel(
    amplitude,
    station_sub,
    beam_sub,
    start,
    turns_ref,
    taps_ref,
    cos_ref,
    sin_ref,
    own_ref,
    next_ref,
    out_ref,
    table,
    wide,
    half,
    filtered,
    spec,
    x_ref,
    w_ref,
    delay_ref,
    members,
    counts,
):
    tap_count, fine = taps_ref.shape
    stations = own_ref.shape[2]
    samples = own_ref.shape[3]
    beams, frames = out_ref.shape[2:4]
    groups = frames // 4
    parts = fine // LANES
    row = stations + UNROLL
    chan = pl.program_id(0)

    @pl.when(chan == 0)
    def _():
        for sub in range(SUBARRAYS):
            def add(s, n, sub=sub):
                members[sub * row + n] = s
                return n + jnp.where(station_sub[s] == sub, 1, 0)

            count = lax.fori_loop(0, stations, add, jnp.int32(0))
            for extra in range(UNROLL):
                members[sub * row + count + extra] = stations
            counts[sub] = (count + UNROLL - 1) // UNROLL
        for part in range(2 * parts):
            x_ref[part, stations] = jnp.zeros((frames, LANES), jnp.float32)
            w_ref[part, pl.ds(stations, 8), :] = jnp.zeros((8, LANES), jnp.float32)
        for b in range(beams):
            delay_ref[b] = jnp.broadcast_to(turns_ref[:, b : b + 1], (stations, LANES))
        cosine = cos_ref[...].astype(jnp.float32)
        sine = sin_ref[...].astype(jnp.float32)
        k = lax.broadcasted_iota(jnp.int32, (fine, fine), 1)
        for phase in range(4):
            q = (3 * phase * k) & 3
            cq = jnp.where(q == 0, 1.0, jnp.where(q == 2, -1.0, 0.0))
            sq = jnp.where(q == 1, 1.0, jnp.where(q == 3, -1.0, 0.0))
            same = (cosine * cq - sine * sq).astype(jnp.bfloat16)
            cross = sine * cq + cosine * sq
            table[phase, 0:fine, 0:fine] = same
            table[phase, fine:, fine:] = same
            table[phase, fine:, 0:fine] = cross.astype(jnp.bfloat16)
            table[phase, 0:fine, fine:] = (-cross).astype(jnp.bfloat16)

    for ri in range(2):
        wide[ri, :, 0:samples] = own_ref[ri, 0].astype(jnp.float32)
        wide[ri, :, samples:] = next_ref[ri, 0].astype(jnp.float32)
        shift = fine // 4
        length = half.shape[2]
        half[ri] = wide[ri, :, shift : shift + length]

    hop = 3 * fine // 4

    @pl.loop(0, groups)
    def _(g):
        for phase in range(4):
            source = wide if phase % 2 == 0 else half
            base = phase * hop - (0 if phase % 2 == 0 else fine // 4)
            for ri in range(2):
                total = None
                for tap in range(tap_count):
                    at = pl.multiple_of(g * 3 * fine + (base + tap * fine), LANES)
                    term = taps_ref[tap : tap + 1, :] * source[ri, :, pl.ds(at, fine)]
                    total = term if total is None else total + term
                filtered[phase, pl.ds(pl.multiple_of(g * stations, stations), stations), ri * fine : (ri + 1) * fine] = (
                    total.astype(jnp.bfloat16)
                )

    for phase in range(4):
        result = jnp.dot(filtered[phase], table[phase], preferred_element_type=jnp.float32)
        for g in range(groups):
            at = (4 * g + phase) * stations
            for part in range(2 * parts):
                spec[part, at : at + stations, :] = result[
                    g * stations : (g + 1) * stations, part * LANES : (part + 1) * LANES
                ]
    for s in range(stations):
        for part in range(2 * parts):
            x_ref[part, s] = spec.at[part][pl.ds(s, frames, stride=stations), :]

    lane = lax.broadcasted_iota(jnp.int32, (stations, LANES), 1)
    first = (start[0] + chan) * fine

    @pl.loop(0, beams)
    def _(b):
        delay = delay_ref[b]
        for part in range(parts):
            turn = (delay * (lane + (first + part * LANES))) & 65535
            c, s = unit_turn(turn)
            w_ref[part, 0:stations, :] = c * amplitude
            w_ref[parts + part, 0:stations, :] = s * (-amplitude)
        sub = beam_sub[b]

        def add(i, carry):
            totals = list(carry)
            for u in range(UNROLL):
                s = members[sub * row + i * UNROLL + u]
                for part in range(parts):
                    w_re = w_ref.at[part][pl.ds(s, 8, stride=0), :][None]
                    w_im = w_ref.at[parts + part][pl.ds(s, 8, stride=0), :][None]
                    x_re = x_ref[part, s].reshape(frames // 8, 8, LANES)
                    x_im = x_ref[parts + part, s].reshape(frames // 8, 8, LANES)
                    totals[part] = totals[part] + (w_re * x_re - w_im * x_im)
                    totals[parts + part] = totals[parts + part] + (w_re * x_im + w_im * x_re)
            return tuple(totals)

        zero = jnp.zeros((frames // 8, 8, LANES), jnp.float32)
        totals = lax.fori_loop(0, counts[sub], add, (zero,) * (2 * parts))
        for part in range(parts):
            lanes = slice(part * LANES, (part + 1) * LANES)
            out_ref[0, 0, b, :, lanes] = totals[part].reshape(frames, LANES).astype(jnp.bfloat16)
            out_ref[0, 1, b, :, lanes] = totals[parts + part].reshape(frames, LANES).astype(jnp.bfloat16)


def beam_sums(own, following, taps, delays, station_sub, beam_sub, chan_start, amplitude):
    tap_count, fine = taps.shape
    chans, stations, samples = own.shape[1:]
    beams = delays.shape[0]
    hop = 3 * fine // 4
    frames = samples // hop
    parts = fine // LANES
    cosine, sine = dft_tables(fine)
    whole = lambda *shape: pl.BlockSpec(shape, lambda c, *_: (0,) * len(shape))
    volts_spec = pl.BlockSpec((2, 1, stations, samples), lambda c, *_: (0, c, 0, 0))
    length = 2 * samples - LANES
    return pl.pallas_call(
        functools.partial(beam_kernel, amplitude),
        out_shape=jax.ShapeDtypeStruct((chans, 2, beams, frames, fine), jnp.bfloat16),
        grid_spec=pltpu.PrefetchScalarGridSpec(
            num_scalar_prefetch=3,
            grid=(chans,),
            in_specs=[
                whole(stations, beams),
                whole(tap_count, fine),
                whole(fine, fine),
                whole(fine, fine),
                volts_spec,
                volts_spec,
            ],
            out_specs=pl.BlockSpec((1, 2, beams, frames, fine), lambda c, *_: (c, 0, 0, 0, 0)),
            scratch_shapes=[
                pltpu.VMEM((4, 2 * fine, 2 * fine), jnp.bfloat16),
                pltpu.VMEM((2, stations, 2 * samples), jnp.float32),
                pltpu.VMEM((2, stations, length), jnp.float32),
                pltpu.VMEM((4, frames // 4 * stations, 2 * fine), jnp.bfloat16),
                pltpu.VMEM((2 * parts, (frames + 1) * stations, LANES), jnp.float32),
                pltpu.VMEM((2 * parts, stations + 1, frames, LANES), jnp.float32),
                pltpu.VMEM((2 * parts, stations + 8, LANES), jnp.float32),
                pltpu.VMEM((beams, stations, LANES), jnp.int32),
                pltpu.SMEM((SUBARRAYS * (stations + UNROLL),), jnp.int32),
                pltpu.SMEM((SUBARRAYS,), jnp.int32),
            ],
        ),
        compiler_params=pltpu.CompilerParams(
            dimension_semantics=("arbitrary",), vmem_limit_bytes=VMEM_LIMIT
        ),
        name="beam_sums",
    )(station_sub, beam_sub, chan_start, delays.T, taps, cosine, sine, own, following)


def exchange_kernel(sizes, part_ref, out_ref, *scratch):
    n_chan, n_core, bits = sizes
    received, sent = scratch[:bits], scratch[bits : 2 * bits - 1]
    total, send, recv, far_send, far_recv, own_sem = scratch[2 * bits - 1 :]
    chans = part_ref.shape[0]
    per_device = total.shape[3]
    stn, chan, core = (lax.axis_index(name) for name in ("stn", "chan", "beam"))
    own_bit = [(stn // 2 ** (bits - 1 - dim)) % 2 for dim in range(bits)]
    orders = (tuple(range(bits - 1, -1, -1)), tuple(range(bits)))

    def partner(dim):
        return (stn + (1 - 2 * own_bit[dim]) * 2 ** (bits - 1 - dim), chan, core)

    def far(dz, dc):
        return ((chan + dz) % n_chan, (core + dc) % n_core)

    offsets = [(dz, dc) for dz in range(n_chan) for dc in range(n_core)]
    barrier = pltpu.get_barrier_semaphore()
    peers = [partner(dim) for dim in range(bits)] + [(stn, *far(dz, dc)) for dz, dc in offsets[1:]]
    for peer in peers:
        pl.semaphore_signal(barrier, inc=1, device_id=peer, device_id_type=MESH)
    pl.semaphore_wait(barrier, len(peers))

    def region(ri, stage, last):
        order = orders[ri]
        index = [slice(None)] * bits
        for dim in order[:stage]:
            index[dim] = own_bit[dim]
        if stage < bits:
            index[order[stage]] = last(order[stage])
        return index

    def other(dim):
        return 1 - own_bit[dim]

    def with_received(c, ri, stage, index):
        value = part_ref[(c, ri, *index)].astype(jnp.float32)
        for earlier in range(stage):
            kept = [dim for dim in range(bits) if dim not in orders[ri][: earlier + 1]]
            piece = received[earlier][(c, ri, *(index[dim] for dim in kept))]
            value = value + piece.astype(jnp.float32)
        return value

    def hop(c, ri, stage):
        if stage == 0:
            source = part_ref.at[(c, ri, *region(ri, 0, other))]
        else:
            source = sent[stage - 1].at[c, ri]
        return pltpu.make_async_remote_copy(
            src_ref=source,
            dst_ref=received[stage].at[c, ri],
            send_sem=send.at[stage, c, ri],
            recv_sem=recv.at[stage, c, ri],
            device_id=partner(orders[ri][stage]),
            device_id_type=MESH,
        )

    def deliver(c, number):
        z, k = far(*offsets[number])
        return pltpu.make_async_remote_copy(
            src_ref=total.at[c, z, k],
            dst_ref=out_ref.at[:, :, chan * chans + c, core],
            send_sem=far_send.at[c, number],
            recv_sem=far_recv.at[c, number],
            device_id=(stn, z, k),
            device_id_type=MESH,
        )

    def keep(c):
        return pltpu.make_async_copy(
            total.at[c, chan, core], out_ref.at[:, :, chan * chans + c, core], own_sem.at[c]
        )

    def step(c, stage):
        if stage == 0:
            for ri in range(2):
                hop(c, ri, 0).start()
            return
        for ri in range(2):
            hop(c, ri, stage - 1).wait_recv()
            if stage < bits:
                sent[stage - 1][c, ri] = with_received(
                    c, ri, stage, region(ri, stage, other)
                ).astype(jnp.bfloat16)
            else:
                value = with_received(c, ri, stage, own_bit).astype(jnp.bfloat16)
                value = value.reshape((n_chan, n_core, per_device) + value.shape[1:])
                total[c, :, :, :, ri] = value
        if stage < bits:
            for ri in range(2):
                hop(c, ri, stage).start()
        else:
            for number in range(len(offsets) - 1, 0, -1):
                deliver(c, number).start()
            keep(c).start()

    for tick in range(chans + bits):
        for c in reversed(range(chans)):
            if 0 <= tick - c <= bits:
                step(c, tick - c)

    for c in range(chans):
        for ri in range(2):
            for stage in range(bits):
                hop(c, ri, stage).wait_send()
        for number in range(1, len(offsets)):
            deliver(c, number).wait()
        keep(c).wait()


def exchange(partial):
    chans, _, beams, frames, fine = partial.shape
    n_stn, n_chan, n_core = (lax.axis_size(name) for name in ("stn", "chan", "beam"))
    bits = n_stn.bit_length() - 1
    assert n_stn == 2**bits
    per = beams // n_stn
    per_device = per // (n_chan * n_core)
    peers = n_chan * n_core
    block = (per, frames, fine)
    halves = [pltpu.VMEM((chans, 2) + (2,) * (bits - 1 - t) + block, jnp.bfloat16) for t in range(bits)]
    out = pl.pallas_call(
        functools.partial(exchange_kernel, (n_chan, n_core, bits)),
        out_shape=jax.ShapeDtypeStruct(
            (per_device, 2, n_chan * chans, n_core, frames, fine), jnp.bfloat16
        ),
        in_specs=[pl.BlockSpec(memory_space=pltpu.VMEM)],
        out_specs=pl.BlockSpec(memory_space=pl.ANY),
        scratch_shapes=[
            *halves,
            *halves[1:],
            pltpu.VMEM((chans, n_chan, n_core, per_device, 2, frames, fine), jnp.bfloat16),
            pltpu.SemaphoreType.DMA((bits, chans, 2)),
            pltpu.SemaphoreType.DMA((bits, chans, 2)),
            pltpu.SemaphoreType.DMA((chans, peers)),
            pltpu.SemaphoreType.DMA((chans, peers)),
            pltpu.SemaphoreType.DMA((chans,)),
        ],
        compiler_params=pltpu.CompilerParams(
            collective_id=0, has_side_effects=True, vmem_limit_bytes=VMEM_LIMIT
        ),
        name="exchange",
    )(partial.reshape((chans, 2) + (2,) * bits + block))
    return out.reshape(per_device, 2, n_chan * chans, n_core * frames, fine)


def body(volts, taps, delays, station_sub, beam_sub):
    own = jnp.transpose(volts, (0, 2, 1, 3))
    size = lax.axis_size("beam")
    following = lax.ppermute(own, "beam", [(i, i - 1) for i in range(1, size)])
    chans = own.shape[1]
    chan_start = (lax.axis_index("chan") * chans).astype(jnp.int32)[None]
    stations = delays.shape[1] * lax.axis_size("stn")
    amplitude = 1.0 / math.sqrt(stations // SUBARRAYS)
    partial = beam_sums(
        own, following, taps, delays, station_sub, beam_sub, chan_start, amplitude
    )
    return exchange(partial).astype(jnp.float32)


def solution(mesh):
    placed = (P(None, "stn", "chan", "beam"), P(), P(None, "stn"), P("stn"), P())
    return jax.shard_map(
        body,
        mesh=mesh,
        in_specs=placed,
        out_specs=P(("stn", "chan", "beam"), None, None, None, None),
        check_vma=False,
    )
```

profile of v0, /device:TPU:0, one launch (start us, length us, event | category | flops | bytes accessed | tf_op | source)
XLA Modules:
  0.0 75.4 jit_solution(4086279190319873082)
XLA Ops:
  0.0 1.3 %collective-permute-start = (bf16[2,3,32,4608]{3,2,1,0:T(8,128)(2,1)}, bf16[2,3,32,4608]{3,2,1,0:T(8,128)(2,1)S(1)}, u32[]{:S(2)}, u32[]{:S(2)}) collective-permute-start(bf16[2,3,32,4608]{3,2,1,0:T(8,128)(2,1)} %bitcast.8), channel_id=1, source_target_pairs={{1,0},{3,2},{5,4},{7,6},{9,8},{11,10},{13,12},{15,14},{17,16},{19,... | collective-permute-start | bytes 5308424 | tf_op jit(solution)/shard_map/ppermute | solution.py:369
  1.3 0.8 %copy.8 = s32[32,32]{0,1:T(8,128)S(1)} copy(s32[32,32]{1,0:T(8,128)} %param.9) | data formatting | bytes 8192 | tf_op args[2]
  2.1 3.7 %collective-permute-done.next_ref = bf16[2,3,32,4608]{3,2,1,0:T(8,128)(2,1)S(1)} collective-permute-done((bf16[2,3,32,4608]{3,2,1,0:T(8,128)(2,1)}, bf16[2,3,32,4608]{3,2,1,0:T(8,128)(2,1)S(1)}, u32[]{:S(2)}, u32[]{:S(2)}) %collective-permute-start) | collective-permute-done | bytes 1769504 | tf_op jit(solution)/shard_map/ppermute | solution.py:369
  5.8 0.0 copy-start
  5.8 1.5 %copy-done = bf16[2,32,3,4608]{3,1,2,0:T(8,128)(2,1)S(1)} copy-done((bf16[2,32,3,4608]{3,1,2,0:T(8,128)(2,1)S(1)}, bf16[2,32,3,4608]{3,1,2,0:T(8,128)(2,1)}, u32[]{:S(2)}) %copy-start) | copy-done | bytes 1769496
  7.3 0.0 copy-start.1
  7.3 0.9 %copy-done.1 = bf16[256,256]{1,0:T(8,128)(2,1)S(1)} copy-done((bf16[256,256]{1,0:T(8,128)(2,1)S(1)}, bf16[256,256]{1,0:T(8,128)(2,1)}, u32[]{:S(2)}) %copy-start.1) | copy-done | bytes 131096
  8.2 0.0 copy-start.2
  8.2 0.9 %copy-done.2 = bf16[256,256]{1,0:T(8,128)(2,1)S(1)} copy-done((bf16[256,256]{1,0:T(8,128)(2,1)S(1)}, bf16[256,256]{1,0:T(8,128)(2,1)}, u32[]{:S(2)}) %copy-start.2) | copy-done | bytes 131096
  9.1 0.0 copy-start.3
  9.1 0.7 copy-done.3
  9.8 0.0 copy-start.4
  9.8 0.7 copy-done.4
  10.4 0.0 copy-start.5
  10.4 0.7 copy-done.5
  11.1 27.1 %beam_sums.1 = bf16[3,2,32,24,256]{4,3,2,1,0:T(8,128)(2,1)S(1)} custom-call(s32[32]{0:T(128)S(1)} %copy-done.4, s32[32]{0:T(128)S(1)} %copy-done.5, s32[1]{0:T(128)} %bitcast.start, s32[32,32]{1,0:T(8,128)S(1)} %bitcast.10, f32[16,256]{1,0:T(8,128)S(1)} %copy-done.3, bf16[256,256]{1,0:T(8,128)(2,1)S(1)} %copy-done.2, bf16[256,256]{1,0:T(8,128)(2,1)S(1)} %copy-done.1, ...), custom_call_target="tpu_custom_call" | custom-call | tf_op jit(solution)/shard_map/beam_sums/pallas_call | solution.py:186
  38.2 36.0 %exchange.1 = bf16[1,2,12,2,24,256]{5,4,3,2,1,0:T(8,128)(2,1)S(1)} custom-call(bf16[3,2,2,2,8,24,256]{6,5,4,3,2,1,0:T(8,128)(2,1)S(1)} %bitcast.7), custom_call_target="tpu_custom_call" | custom-call | tf_op jit(solution)/shard_map/exchange/pallas_call | solution.py:341
  74.2 1.2 %bitcast_convert_fusion = f32[1,2,12,48,256]{4,3,2,1,0:T(8,128)} fusion(bf16[1,2,12,2,24,256]{5,4,3,2,1,0:T(8,128)(2,1)S(1)} %exchange.1), kind=kLoop, calls=%fused_computation | loop fusion | flops 294912 | bytes 1769472 | tf_op jit(solution)/shard_map/convert_element_type | solution.py:377
Async XLA Ops:
  0.0 5.8 %collective-permute-start = (bf16[2,3,32,4608]{3,2,1,0:T(8,128)(2,1)}, bf16[2,3,32,4608]{3,2,1,0:T(8,128)(2,1)S(1)}, u32[]{:S(2)}, u32[]{:S(2)}) collective-permute-start(bf16[2,3,32,4608]{3,2,1,0:T(8,128)(2,1)} %bitcast.8), channel_id=1, source_target_pairs={{1,0},{3,2},{5,4},{7,6},{9,8},{11,10},{13,12},{15,14},{17,16},{19,... | collective-permute-start | bytes 5308424 | tf_op jit(solution)/shard_map/ppermute | solution.py:369
  5.8 1.5 %copy-start = (bf16[2,32,3,4608]{3,1,2,0:T(8,128)(2,1)S(1)}, bf16[2,32,3,4608]{3,1,2,0:T(8,128)(2,1)}, u32[]{:S(2)}) copy-start(bf16[2,32,3,4608]{3,1,2,0:T(8,128)(2,1)} %param.7) | copy-start | bytes 5308420
  7.3 0.9 %copy-start.1 = (bf16[256,256]{1,0:T(8,128)(2,1)S(1)}, bf16[256,256]{1,0:T(8,128)(2,1)}, u32[]{:S(2)}) copy-start(bf16[256,256]{1,0:T(8,128)(2,1)} %constant.13.clone.sin_ref) | copy-start | bytes 393220
  8.2 0.9 %copy-start.2 = (bf16[256,256]{1,0:T(8,128)(2,1)S(1)}, bf16[256,256]{1,0:T(8,128)(2,1)}, u32[]{:S(2)}) copy-start(bf16[256,256]{1,0:T(8,128)(2,1)} %constant.12.clone.cos_ref) | copy-start | bytes 393220
  9.1 0.7 copy-start.3
  9.8 0.7 copy-start.4
  10.4 0.7 copy-start.5
where the time goes:
time: 75.8 us; the launch traced here: 75.4 us
  Pallas kernels  63.1 us (83%)
  local copies, waits for them, and re-layouts  6.1 us (8%)
  waiting for transfers between devices  3.7 us (5%)
  starting transfers between devices  1.28 us (2%)
  other arithmetic  1.18 us (2%)
    pallas_call x1, Pallas kernels, exchange(): pl.pallas_call(functools.partial(exchange_kernel, (n_chan, n_core, bits))...  36 us
    pallas_call x1, Pallas kernels, beam_sums(): pl.pallas_call(functools.partial(beam_kernel, amplitude), out_shape=jax.S...  27.1 us
    unnamed x13, local copies, waits for them, and re-layouts  6.1 us
    ppermute x1, waiting for transfers between devices, body(): following = lax.ppermute(own, 'beam', [(i, i - 1) for i in range(1, size)])  3.7 us
  transfers between devices with their start and end apart: 1, of which 1 were waited for; matrix products, arithmetic and copies ran while one was open for 1% of the time, Pallas kernels for 0%

commit v1 on v0

v1 whole, which is shorter than its diff:
```python
import functools
import math

import jax
import jax.numpy as jnp
import numpy as np
from jax import lax
from jax.experimental import pallas as pl
from jax.experimental.pallas import tpu as pltpu
from jax.sharding import PartitionSpec as P

SUBARRAYS = 4
LANES = 128
QUAD = 4
PHASES = 4
VMEM_LIMIT = 56 * 2**20
MESH = pl.DeviceIdType.MESH


def dft_table(fine, lane_groups):
    index = np.arange(fine)
    angle = 2.0 * np.pi * (index[:, None] * index[None, :] % fine) / fine
    scale = 1.0 / math.sqrt(fine)
    cosine = np.cos(angle) * scale
    sine = np.sin(angle) * scale
    whole = np.stack([np.concatenate([cosine, sine]), np.concatenate([-sine, cosine])])
    halves = []
    for half in range(fine // LANES):
        k = half * LANES + (np.arange(LANES).reshape(-1, lane_groups).T).reshape(-1)
        halves.append(np.concatenate([whole[0][:, k].T, whole[1][:, k].T]))
    return jnp.asarray(np.stack(halves), jnp.bfloat16)


def unit_turn(turn):
    quarter = (turn + 8192) >> 14
    t = (turn - (quarter << 14)).astype(jnp.float32) * (2.0 * math.pi / 65536.0)
    u = t * t
    sine = t * (1.0 + u * (-1.0 / 6 + u * (1.0 / 120 + u * (-1.0 / 5040))))
    cosine = 1.0 + u * (-0.5 + u * (1.0 / 24 + u * (-1.0 / 720 + u * (1.0 / 40320))))
    odd = (quarter & 1) == 1
    c = jnp.where(odd, sine, cosine)
    s = jnp.where(odd, cosine, sine)
    c = jnp.where(((quarter + 1) & 2) == 2, -c, c)
    s = jnp.where((quarter & 2) == 2, -s, s)
    return c, s


def swap_index_with_lanes(tiles, block):
    lane = lax.broadcasted_iota(jnp.int32, tiles[0].shape, 1)
    bit = 1
    while bit < len(tiles):
        upper = (lane & (bit * block)) != 0
        swapped = list(tiles)
        for i in range(len(tiles)):
            if not i & bit:
                low, high = tiles[i], tiles[i | bit]
                swapped[i] = jnp.where(upper, pltpu.roll(high, bit * block, 1), low)
                swapped[i | bit] = jnp.where(upper, high, pltpu.roll(low, LANES - bit * block, 1))
        tiles = swapped
        bit *= 2
    return tiles


def kernel(
    sizes,
    amplitude,
    own_ref,
    taps_hbm,
    table_hbm,
    delays_hbm,
    station_hbm,
    beam_hbm,
    out_ref,
    volts,
    taps_ref,
    table,
    delay_in,
    station_in,
    beam_in,
    wide_taps,
    wide_int,
    member,
    steps,
    state,
    filtered,
    spectra,
    total_ref,
    turned,
    part,
    final,
    own_sem,
    small_sem,
    halo_send,
    halo_recv,
    send,
    recv,
    far_send,
    far_recv,
    keep_sem,
    *exchanged,
):
    n_chan, n_core, bits = sizes
    received, sent = exchanged[:bits], exchanged[bits:]
    chans, stations, samples = own_ref.shape[1:]
    tap_count, fine = taps_ref.shape
    beams = delay_in.shape[0]
    frames = final.shape[-2]
    halves = fine // LANES
    chunks = chans * halves
    lane_groups = LANES // stations
    hop = 3 * fine // 4
    groups = frames // PHASES
    quads = LANES // lane_groups // QUAD
    n_stn = 2**bits
    rows = 2 * beams // n_stn
    per = beams // n_stn
    width = frames * lane_groups
    tiles = QUAD * width // LANES
    halo = volts.shape[3] - samples
    stn, chan, core = (lax.axis_index(name) for name in ("stn", "chan", "beam"))

    def fetch(c):
        return pltpu.make_async_copy(
            own_ref.at[:, c], volts.at[:, c, :, pl.ds(0, samples)], own_sem.at[c]
        )

    small = [
        pltpu.make_async_copy(source, target, small_sem.at[i])
        for i, (source, target) in enumerate(
            (
                (taps_hbm, taps_ref),
                (delays_hbm, delay_in),
                (station_hbm, station_in),
                (beam_hbm, beam_in),
                (table_hbm, table),
            )
        )
    ]
    for copy in small:
        copy.start()
    for c in range(chans):
        fetch(c).start()

    own_bit = [(stn // 2 ** (bits - 1 - dim)) % 2 for dim in range(bits)]
    orders = (tuple(range(bits - 1, -1, -1)), tuple(range(bits)))

    def partner(dim):
        return (stn + (1 - 2 * own_bit[dim]) * 2 ** (bits - 1 - dim), chan, core)

    def far(dz, dc):
        return ((chan + dz) % n_chan, (core + dc) % n_core)

    offsets = [(dz, dc) for dz in range(n_chan) for dc in range(n_core)]
    barrier = pltpu.get_barrier_semaphore()
    peers = [partner(dim) for dim in range(bits)] + [(stn, *far(dz, dc)) for dz, dc in offsets[1:]]
    for peer in peers:
        pl.semaphore_signal(barrier, inc=1, device_id=peer, device_id_type=MESH)
    pl.semaphore_wait(barrier, len(peers))

    def halo_copy(c):
        return pltpu.make_async_remote_copy(
            src_ref=own_ref.at[:, c, :, pl.ds(0, halo)],
            dst_ref=volts.at[:, c, :, pl.ds(samples, halo)],
            send_sem=halo_send.at[c],
            recv_sem=halo_recv.at[c],
            device_id=(stn, chan, core - 1),
            device_id_type=MESH,
        )

    @pl.when(core > 0)
    def _():
        for c in range(chans):
            halo_copy(c).start()

    @pl.when(core == n_core - 1)
    def _():
        volts[:, :, :, samples:] = jnp.zeros((2, chans, stations, halo), volts.dtype)

    for copy in small:
        copy.wait()

    for phase in range(PHASES):
        shift = hop * phase % fine
        rolled = taps_ref[...]
        if shift:
            rolled = pltpu.roll(rolled, shift, 1)
        column = lax.broadcasted_iota(jnp.int32, (1, fine), 1)
        for u in range(tap_count + 1):
            late = rolled[u : u + 1] if u < tap_count else jnp.zeros((1, fine), jnp.float32)
            early = rolled[u - 1 : u] if u > 0 else jnp.zeros((1, fine), jnp.float32)
            row = jnp.where(column >= shift, late, early)
            wide_taps[phase, u] = jnp.broadcast_to(row, (16, fine)).astype(jnp.bfloat16)

    def widened(value, count):
        wide_int[...] = jnp.zeros(wide_int.shape, jnp.int32)
        wide_int[0:count, 0:stations] = value
        full = wide_int[...]
        step = stations
        while step < LANES:
            full = full + pltpu.roll(full, step, 1)
            step *= 2
        return full[0:count]

    group_of_lane = lax.broadcasted_iota(jnp.int32, (1, LANES), 1) // stations
    station_row = widened(station_in[...], 1).astype(jnp.float32)
    square = (beams, beams)
    diagonal = lax.broadcasted_iota(jnp.int32, square, 0) == lax.broadcasted_iota(jnp.int32, square, 1)
    beam_row = jnp.broadcast_to(beam_in[...].astype(jnp.float32), square)
    beam_column = jnp.sum(jnp.where(diagonal, beam_row, 0.0), axis=1, keepdims=True)
    member[...] = jnp.where(beam_column == station_row, amplitude, 0.0)
    delay = widened(delay_in[...], beams)
    wide_int[...] = delay
    for i, stride in enumerate((lane_groups, QUAD * lane_groups)):
        c, s = unit_turn((delay * stride) & 65535)
        steps[i, 0] = c
        steps[i, 1] = -s

    def filter_channel(c):
        @pl.loop(0, 2)
        def _(ri):
            for half in range(halves):
                for phase in range(PHASES):
                    shift = hop * phase % fine
                    block0 = hop * phase // fine
                    first = 0 if shift < (half + 1) * LANES else 1
                    last = tap_count - 1 if shift <= half * LANES else tap_count
                    lanes = slice(half * LANES, (half + 1) * LANES)
                    taps = {
                        u: wide_taps[phase, u, :, lanes][None] for u in range(first, last + 1)
                    }
                    sums = [[None, None] for _ in range(groups)]
                    for block in range(block0 + first, block0 + last + 1 + 3 * (groups - 1)):
                        at = block * fine + half * LANES
                        value = volts[ri, c, :, at : at + LANES].reshape(stations // 16, 16, LANES)
                        for g in range(groups):
                            u = block - block0 - 3 * g
                            if first <= u <= last:
                                term = taps[u] * value
                                so_far = sums[g][u % 2]
                                sums[g][u % 2] = term if so_far is None else so_far + term
                    for g in range(groups):
                        f = PHASES * g + phase
                        filtered[
                            f * stations : (f + 1) * stations,
                            pl.ds(pl.multiple_of(ri * fine + half * LANES, LANES), LANES),
                        ] = (sums[g][0] + sums[g][1]).reshape(stations, LANES)

    def transform(half):
        @pl.loop(0, frames // lane_groups)
        def _(fb):
            rhs = filtered[pl.ds(pl.multiple_of(fb * LANES, LANES), LANES), :]
            result = lax.dot_general(
                table[half], rhs, (((1,), (1,)), ((), ())), preferred_element_type=jnp.float32
            )
            count = LANES // lane_groups
            for ri in range(2):
                pieces = [
                    result[(ri * lane_groups + j) * count : (ri * lane_groups + j + 1) * count]
                    for j in range(lane_groups)
                ]
                for j, piece in enumerate(swap_index_with_lanes(pieces, stations)):
                    at = pl.multiple_of((fb * lane_groups + j) * count, count)
                    spectra[ri, pl.ds(at, count), :] = piece

    def form_beams(chunk, c, half):
        count = LANES // lane_groups
        frequency = (chan * chans + c) * fine + half * LANES + group_of_lane
        cosine, sine = unit_turn((wide_int[...] * frequency) & 65535)
        state[0] = cosine * member[...]
        state[1] = -sine * member[...]
        lane = lax.broadcasted_iota(jnp.int32, (frames, LANES), 1) // stations
        out_lane = lax.broadcasted_iota(jnp.int32, (2 * beams, LANES), 1)

        def times(a, i):
            e_re, e_im = steps[i, 0], steps[i, 1]
            return (a[0] * e_re - a[1] * e_im, a[0] * e_im + a[1] * e_re)

        def stacked(top, bottom):
            both = [v.reshape(n_stn, per, LANES) for v in (top, bottom)]
            return jnp.stack(both, axis=1).reshape(2 * beams, LANES)

        @pl.loop(0, quads)
        def _(quad):
            first = weight = (state[0], state[1])
            outs = []
            for q in range(QUAD):
                if q:
                    weight = times(weight, 0)
                w_re, w_im = weight
                lhs = jnp.concatenate([stacked(w_re, w_im), stacked(-w_im, w_re)], axis=1)
                at = quad * QUAD + q
                x = [spectra.at[ri][pl.ds(at, frames, stride=count), :] for ri in range(2)]
                blocks = [
                    jnp.concatenate([jnp.where(lane == j, v, 0.0) for v in x], axis=1)
                    for j in range(lane_groups)
                ]
                if width < LANES:
                    blocks.append(jnp.zeros((LANES - width, 2 * LANES), jnp.float32))
                rhs = jnp.concatenate(blocks, axis=0)
                result = lax.dot_general(
                    lhs.astype(jnp.bfloat16),
                    rhs.astype(jnp.bfloat16),
                    (((1,), (1,)), ((), ())),
                    preferred_element_type=jnp.float32,
                )
                turn = q * width % LANES
                outs.append(pltpu.roll(result, turn, 1) if turn else result)
            following = times(first, 1)
            state[0] = following[0]
            state[1] = following[1]
            for t in range(tiles):
                value = None
                for q in range(QUAD):
                    start = q * width - t * LANES
                    if -width < start < LANES:
                        value = outs[q] if value is None else jnp.where(out_lane >= start, outs[q], value)
                value = value.astype(jnp.bfloat16)
                for d in range(n_stn):
                    place = [(d >> (bits - 1 - dim)) & 1 for dim in range(bits)]
                    part[(chunk, quad // (quads // 2), *place, quad % (quads // 2), t)] = value[
                        d * rows : (d + 1) * rows
                    ]

    def region(order, stage, last):
        index = [slice(None)] * bits
        for dim in orders[order][:stage]:
            index[dim] = own_bit[dim]
        if stage < bits:
            index[orders[order][stage]] = last(orders[order][stage])
        return index

    def other(dim):
        return 1 - own_bit[dim]

    def with_received(chunk, order, stage, index):
        value = part[(chunk, order, *index)].astype(jnp.float32)
        for earlier in range(stage):
            kept = [dim for dim in range(bits) if dim not in orders[order][: earlier + 1]]
            piece = received[earlier][(chunk, order, *(index[dim] for dim in kept))]
            value = value + piece.astype(jnp.float32)
        return value

    def hop_copy(chunk, order, stage):
        if stage == 0:
            source = part.at[(chunk, order, *region(order, 0, other))]
        else:
            source = sent[stage - 1].at[chunk, order]
        return pltpu.make_async_remote_copy(
            src_ref=source,
            dst_ref=received[stage].at[chunk, order],
            send_sem=send.at[stage, chunk, order],
            recv_sem=recv.at[stage, chunk, order],
            device_id=partner(orders[order][stage]),
            device_id_type=MESH,
        )

    def place_of(chunk):
        c = chunk // halves
        lanes = pl.ds(pl.multiple_of((chunk % halves) * LANES, LANES), LANES)
        return out_ref.at[:, :, chan * chans + c, core, :, lanes]

    def deliver(chunk, number):
        z, k = far(*offsets[number])
        return pltpu.make_async_remote_copy(
            src_ref=final.at[chunk, z, k],
            dst_ref=place_of(chunk),
            send_sem=far_send.at[chunk, number],
            recv_sem=far_recv.at[chunk, number],
            device_id=(stn, z, k),
            device_id_type=MESH,
        )

    def keep(chunk):
        return pltpu.make_async_copy(final.at[chunk, chan, core], place_of(chunk), keep_sem.at[chunk])

    def finish(chunk):
        for order in range(2):
            value = with_received(chunk, order, bits, own_bit)
            for quad in range(quads // 2):
                at = (order * (quads // 2) + quad) * rows
                for t in range(tiles):
                    total_ref[t, at : at + rows, :] = value[quad, t]
        for t in range(tiles):
            turned[t * LANES : (t + 1) * LANES, :] = total_ref[t].T
        pieces = [turned[i * frames : (i + 1) * frames, :] for i in range(rows)]
        for row, piece in enumerate(swap_index_with_lanes(pieces, 1)):
            ri, b = divmod(row, per)
            device, at = divmod(b, per // (n_chan * n_core))
            z, k = divmod(device, n_core)
            final[chunk, z, k, at, ri] = piece.astype(jnp.bfloat16)

    def step(chunk, stage):
        for order in range(2):
            hop_copy(chunk, order, stage - 1).wait_recv()
            if stage < bits:
                sent[stage - 1][chunk, order] = with_received(
                    chunk, order, stage, region(order, stage, other)
                ).astype(jnp.bfloat16)
                hop_copy(chunk, order, stage).start()
        if stage == bits:
            finish(chunk)
            for number in range(len(offsets) - 1, 0, -1):
                deliver(chunk, number).start()
            keep(chunk).start()

    @pl.loop(0, chunks + bits)
    def _(tick):
        @pl.when(tick < chunks)
        def _():
            c = tick // halves
            half = tick % halves

            @pl.when(half == 0)
            def _():
                fetch(c).wait()

                @pl.when(core < n_core - 1)
                def _():
                    halo_copy(c).wait_recv()

                filter_channel(c)

            transform(half)
            form_beams(tick, c, half)
            for order in range(2):
                hop_copy(tick, order, 0).start()

        for stage in range(1, bits + 1):
            chunk = tick - stage

            @pl.when((chunk >= 0) & (chunk < chunks))
            def _(chunk=chunk, stage=stage):
                step(chunk, stage)

    @pl.when(core > 0)
    def _():
        for c in range(chans):
            halo_copy(c).wait_send()

    @pl.loop(0, chunks)
    def _(chunk):
        for order in range(2):
            for stage in range(bits):
                hop_copy(chunk, order, stage).wait_send()
        for number in range(1, len(offsets)):
            deliver(chunk, number).wait()
        keep(chunk).wait()


def body(volts, taps, delays, station_sub, beam_sub):
    own = jnp.transpose(volts, (0, 2, 1, 3))
    chans, stations, samples = own.shape[1:]
    tap_count, fine = taps.shape
    beams = delays.shape[0]
    n_stn, n_chan, n_core = (lax.axis_size(name) for name in ("stn", "chan", "beam"))
    bits = n_stn.bit_length() - 1
    hop = 3 * fine // 4
    frames = samples // hop
    per = beams // n_stn
    per_device = per // (n_chan * n_core)
    halves = fine // LANES
    chunks = chans * halves
    lane_groups = LANES // stations
    quads = LANES // lane_groups // QUAD
    tiles = QUAD * frames * lane_groups // LANES
    rows = 2 * per
    peers = n_chan * n_core
    assert n_stn == 2**bits and rows == QUAD * lane_groups and quads * rows == LANES
    assert QUAD * frames * lane_groups == tiles * LANES and frames * lane_groups <= LANES
    blocks = hop * (PHASES - 1) // fine + tap_count + 1 + 3 * (frames // PHASES - 1)
    amplitude = 1.0 / math.sqrt(stations * n_stn // SUBARRAYS)
    block = (quads // 2, tiles, rows, LANES)
    pieces = [
        pltpu.VMEM((chunks, 2) + (2,) * (bits - 1 - t) + block, jnp.bfloat16) for t in range(bits)
    ]
    hbm = pl.BlockSpec(memory_space=pltpu.HBM)
    dma = pltpu.SemaphoreType.DMA
    out = pl.pallas_call(
        functools.partial(kernel, (n_chan, n_core, bits), amplitude),
        out_shape=jax.ShapeDtypeStruct(
            (per_device, 2, n_chan * chans, n_core, frames, fine), jnp.bfloat16
        ),
        in_specs=[hbm] * 6,
        out_specs=pl.BlockSpec(memory_space=pl.ANY),
        scratch_shapes=[
            pltpu.VMEM((2, chans, stations, blocks * fine), jnp.bfloat16),
            pltpu.VMEM((tap_count, fine), jnp.float32),
            pltpu.VMEM((halves, 2 * LANES, 2 * fine), jnp.bfloat16),
            pltpu.VMEM((beams, stations), jnp.int32),
            pltpu.VMEM((1, stations), jnp.int32),
            pltpu.VMEM((1, beams), jnp.int32),
            pltpu.VMEM((PHASES, tap_count + 1, 16, fine), jnp.bfloat16),
            pltpu.VMEM((beams, LANES), jnp.int32),
            pltpu.VMEM((beams, LANES), jnp.float32),
            pltpu.VMEM((2, 2, beams, LANES), jnp.float32),
            pltpu.VMEM((2, beams, LANES), jnp.float32),
            pltpu.VMEM((frames * stations, 2 * fine), jnp.bfloat16),
            pltpu.VMEM((2, frames * LANES // lane_groups, LANES), jnp.float32),
            pltpu.VMEM((tiles, LANES, LANES), jnp.float32),
            pltpu.VMEM((tiles * LANES, LANES), jnp.float32),
            pltpu.VMEM((chunks, 2) + (2,) * bits + block, jnp.bfloat16),
            pltpu.VMEM((chunks, n_chan, n_core, per_device, 2, frames, LANES), jnp.bfloat16),
            dma((chans,)),
            dma((5,)),
            dma((chans,)),
            dma((chans,)),
            dma((bits, chunks, 2)),
            dma((bits, chunks, 2)),
            dma((chunks, peers)),
            dma((chunks, peers)),
            dma((chunks,)),
            *pieces,
            *pieces[1:],
        ],
        compiler_params=pltpu.CompilerParams(
            collective_id=0, has_side_effects=True, vmem_limit_bytes=VMEM_LIMIT
        ),
        name="channelize_and_beamform",
    )(
        own,
        taps,
        dft_table(fine, lane_groups),
        delays,
        station_sub[None],
        beam_sub[None],
    )
    return out.reshape(per_device, 2, n_chan * chans, n_core * frames, fine).astype(jnp.float32)


def solution(mesh):
    placed = (P(None, "stn", "chan", "beam"), P(), P(None, "stn"), P("stn"), P())
    return jax.shard_map(
        body,
        mesh=mesh,
        in_specs=placed,
        out_specs=P(("stn", "chan", "beam"), None, None, None, None),
        check_vma=False,
    )
```

time: 75.8 us -> 57.7 us (0.76)
  Pallas kernels: 63.1 us -> 55.3 us
  local copies, waits for them, and re-layouts: 6.1 us -> 0 us
  waiting for transfers between devices: 3.7 us -> 0 us
  starting transfers between devices: 1.28 us -> 0 us
  other arithmetic: 1.18 us -> 2.21 us
    pallas_call x2 -> x1, Pallas kernels: 63.1 us -> 55.3 us  [body(): pl.pallas_call(functools.partial(kernel, (n_chan, n_core, bits), amplitud...]
    unnamed x13 -> x0, local copies, waits for them, and re-layouts: 6.1 us -> none
    ppermute x1 -> x0, waiting for transfers between devices: 3.7 us -> none  [body(): following = lax.ppermute(own, 'beam', [(i, i - 1) for i in range(1, size)])]
    ppermute x1 -> x0, starting transfers between devices: 1.28 us -> none  [body(): following = lax.ppermute(own, 'beam', [(i, i - 1) for i in range(1, size)])]
    convert_element_type x1, other arithmetic: 1.18 us -> 2.21 us  [body(): out.reshape(per_device, 2, n_chan * chans, n_core * frames, fine)]
  transfers between devices with their start and end apart: 1 -> 0, of which waited for: 1 -> 0; matrix products, arithmetic and copies ran while one was open for 1% -> 0% of each run, Pallas kernels for 0% -> 0%
where the time goes in v1:
time: 57.7 us; the launch traced here: 57.5 us
  Pallas kernels  55.3 us (96%)
  other arithmetic  2.21 us (4%)
    pallas_call x1, Pallas kernels, body(): pl.pallas_call(functools.partial(kernel, (n_chan, n_core, bits), amplitud...  55.3 us
    convert_element_type x1, other arithmetic, body(): out.reshape(per_device, 2, n_chan * chans, n_core * frames, fine)  2.21 us

profile of v1, /device:TPU:0, one launch (start us, length us, event | category | flops | bytes accessed | tf_op | source)
XLA Modules:
  0.0 57.5 jit_solution(9311263976673870778)
XLA Ops:
  0.0 55.3 %channelize_and_beamform.1 = bf16[1,2,12,2,24,256]{5,4,3,2,1,0:T(8,128)(2,1)} custom-call(bf16[2,3,32,4608]{3,2,1,0:T(8,128)(2,1)} %bitcast.6, f32[16,256]{1,0:T(8,128)} %taps_hbm.1, bf16[2,256,512]{2,1,0:T(8,128)(2,1)} %constant.2.clone.table_hbm, s32[32,32]{1,0:T(8,128)} %delays_hbm.1, s32[1,32]{1,0:T(1,128)} %bitcast.7, s32[1,32]{1,0:T(1,128)} %bitcast.8), custom_call_target="tpu_custom_call" | custom-call | tf_op jit(solution)/shard_map/channelize_and_beamform/pallas_call | solution.py:478
  55.3 2.2 %bitcast_convert_fusion = f32[1,2,12,48,256]{4,3,2,1,0:T(8,128)} fusion(bf16[1,2,12,2,24,256]{5,4,3,2,1,0:T(8,128)(2,1)} %channelize_and_beamform.1), kind=kLoop, calls=%fused_computation | loop fusion | flops 294912 | bytes 1769472 | tf_op jit(solution)/shard_map/convert_element_type | solution.py:527

commit v2 on v1

--- a/solution.py
+++ b/solution.py
@@ -12,6 +12,9 @@
 SUBARRAYS = 4
 LANES = 128
 QUAD = 4
+WIDE = 2
+UNROLL_FB = True
+BEAM_UNROLL = 8
 PHASES = 4
 VMEM_LIMIT = 56 * 2**20
 MESH = pl.DeviceIdType.MESH
@@ -28,7 +31,7 @@
     for half in range(fine // LANES):
         k = half * LANES + (np.arange(LANES).reshape(-1, lane_groups).T).reshape(-1)
         halves.append(np.concatenate([whole[0][:, k].T, whole[1][:, k].T]))
-    return jnp.asarray(np.stack(halves), jnp.bfloat16)
+    return jnp.asarray(np.concatenate(halves), jnp.bfloat16)
 
 
 def unit_turn(turn):
@@ -245,22 +248,35 @@
                             pl.ds(pl.multiple_of(ri * fine + half * LANES, LANES), LANES),
                         ] = (sums[g][0] + sums[g][1]).reshape(stations, LANES)
 
-    def transform(half):
-        @pl.loop(0, frames // lane_groups)
-        def _(fb):
-            rhs = filtered[pl.ds(pl.multiple_of(fb * LANES, LANES), LANES), :]
+    def transform():
+        count = LANES // lane_groups
+
+        def one(fb):
+            rhs = filtered[pl.ds(pl.multiple_of(fb * LANES, LANES), WIDE * LANES), :]
             result = lax.dot_general(
-                table[half], rhs, (((1,), (1,)), ((), ())), preferred_element_type=jnp.float32
+                table[...], rhs, (((1,), (1,)), ((), ())), preferred_element_type=jnp.float32
             )
-            count = LANES // lane_groups
-            for ri in range(2):
-                pieces = [
-                    result[(ri * lane_groups + j) * count : (ri * lane_groups + j + 1) * count]
-                    for j in range(lane_groups)
-                ]
-                for j, piece in enumerate(swap_index_with_lanes(pieces, stations)):
-                    at = pl.multiple_of((fb * lane_groups + j) * count, count)
-                    spectra[ri, pl.ds(at, count), :] = piece
+            for half in range(halves):
+                for ri in range(2):
+                    for sub in range(WIDE):
+                        pieces = [
+                            result[
+                                ((half * 2 + ri) * lane_groups + j) * count : ((half * 2 + ri) * lane_groups + j + 1) * count,
+                                sub * LANES : (sub + 1) * LANES,
+                            ]
+                            for j in range(lane_groups)
+                        ]
+                        for j, piece in enumerate(swap_index_with_lanes(pieces, stations)):
+                            at = pl.multiple_of(((fb + sub) * lane_groups + j) * count, count)
+                            spectra[half, ri, pl.ds(at, count), :] = piece
+
+        if UNROLL_FB:
+            for fb in range(0, frames // lane_groups, WIDE):
+                one(fb)
+        else:
+            @pl.loop(0, frames // lane_groups // WIDE)
+            def _(fb):
+                one(fb * WIDE)
 
     def form_beams(chunk, c, half):
         count = LANES // lane_groups
@@ -279,7 +295,7 @@
             both = [v.reshape(n_stn, per, LANES) for v in (top, bottom)]
             return jnp.stack(both, axis=1).reshape(2 * beams, LANES)
 
-        @pl.loop(0, quads)
+        @pl.loop(0, quads, unroll=BEAM_UNROLL)
         def _(quad):
             first = weight = (state[0], state[1])
             outs = []
@@ -289,13 +305,17 @@
                 w_re, w_im = weight
                 lhs = jnp.concatenate([stacked(w_re, w_im), stacked(-w_im, w_re)], axis=1)
                 at = quad * QUAD + q
-                x = [spectra.at[ri][pl.ds(at, frames, stride=count), :] for ri in range(2)]
+                x = [spectra.at[half, ri][pl.ds(at, frames, stride=count), :] for ri in range(2)]
                 blocks = [
                     jnp.concatenate([jnp.where(lane == j, v, 0.0) for v in x], axis=1)
                     for j in range(lane_groups)
                 ]
                 if width < LANES:
                     blocks.append(jnp.zeros((LANES - width, 2 * LANES), jnp.float32))
+                turn = q * width % LANES
+                if turn:
+                    blocks = [jnp.concatenate(blocks, axis=0)]
+                    blocks = [blocks[0][LANES - turn :], blocks[0][: LANES - turn]]
                 rhs = jnp.concatenate(blocks, axis=0)
                 result = lax.dot_general(
                     lhs.astype(jnp.bfloat16),
@@ -303,8 +323,7 @@
                     (((1,), (1,)), ((), ())),
                     preferred_element_type=jnp.float32,
                 )
-                turn = q * width % LANES
-                outs.append(pltpu.roll(result, turn, 1) if turn else result)
+                outs.append(result)
             following = times(first, 1)
             state[0] = following[0]
             state[1] = following[1]
@@ -419,8 +438,8 @@
                     halo_copy(c).wait_recv()
 
                 filter_channel(c)
-
-            transform(half)
+                transform()
+
             form_beams(tick, c, half)
             for order in range(2):
                 hop_copy(tick, order, 0).start()
@@ -485,7 +504,7 @@
         scratch_shapes=[
             pltpu.VMEM((2, chans, stations, blocks * fine), jnp.bfloat16),
             pltpu.VMEM((tap_count, fine), jnp.float32),
-            pltpu.VMEM((halves, 2 * LANES, 2 * fine), jnp.bfloat16),
+            pltpu.VMEM((halves * 2 * LANES, 2 * fine), jnp.bfloat16),
             pltpu.VMEM((beams, stations), jnp.int32),
             pltpu.VMEM((1, stations), jnp.int32),
             pltpu.VMEM((1, beams), jnp.int32),
@@ -495,7 +514,7 @@
             pltpu.VMEM((2, 2, beams, LANES), jnp.float32),
             pltpu.VMEM((2, beams, LANES), jnp.float32),
             pltpu.VMEM((frames * stations, 2 * fine), jnp.bfloat16),
-            pltpu.VMEM((2, frames * LANES // lane_groups, LANES), jnp.float32),
+            pltpu.VMEM((halves, 2, frames * LANES // lane_groups, LANES), jnp.float32),
             pltpu.VMEM((tiles, LANES, LANES), jnp.float32),
             pltpu.VMEM((tiles * LANES, LANES), jnp.float32),
             pltpu.VMEM((chunks, 2) + (2,) * bits + block, jnp.bfloat16),

time: 57.7 us -> 45.4 us (0.79)
  Pallas kernels: 55.3 us -> 43.1 us
    pallas_call x1, Pallas kernels: 55.3 us -> 43.1 us  [body(): pl.pallas_call(functools.partial(kernel, (n_chan, n_core, bits), amplitud...]
where the time goes in v2:
time: 45.4 us; the launch traced here: 45.3 us
  Pallas kernels  43.1 us (95%)
  other arithmetic  2.21 us (5%)
    pallas_call x1, Pallas kernels, body(): pl.pallas_call(functools.partial(kernel, (n_chan, n_core, bits), amplitud...  43.1 us
    convert_element_type x1, other arithmetic, body(): out.reshape(per_device, 2, n_chan * chans, n_core * frames, fine)  2.21 us

profile of v2, /device:TPU:0, one launch (start us, length us, event | category | flops | bytes accessed | tf_op | source)
XLA Modules:
  0.0 45.3 jit_solution(13323010373464012492)
XLA Ops:
  0.0 43.1 %channelize_and_beamform.1 = bf16[1,2,12,2,24,256]{5,4,3,2,1,0:T(8,128)(2,1)} custom-call(bf16[2,3,32,4608]{3,2,1,0:T(8,128)(2,1)} %bitcast.6, f32[16,256]{1,0:T(8,128)} %taps_hbm.1, bf16[512,512]{1,0:T(8,128)(2,1)} %constant.2.clone.table_hbm, s32[32,32]{1,0:T(8,128)} %delays_hbm.1, s32[1,32]{1,0:T(1,128)} %bitcast.7, s32[1,32]{1,0:T(1,128)} %bitcast.8), custom_call_target="tpu_custom_call" | custom-call | tf_op jit(solution)/shard_map/channelize_and_beamform/pallas_call | solution.py:497
  43.1 2.2 %bitcast_convert_fusion = f32[1,2,12,48,256]{4,3,2,1,0:T(8,128)} fusion(bf16[1,2,12,2,24,256]{5,4,3,2,1,0:T(8,128)(2,1)} %channelize_and_beamform.1), kind=kLoop, calls=%fused_computation | loop fusion | flops 294912 | bytes 1769472 | tf_op jit(solution)/shard_map/convert_element_type | solution.py:546

commit v3 on v2

--- a/solution.py
+++ b/solution.py
@@ -14,9 +14,11 @@
 QUAD = 4
 WIDE = 2
 UNROLL_FB = True
-BEAM_UNROLL = 8
+LEAD = 2
+DELAY = 0
+DRAIN = 3
 PHASES = 4
-VMEM_LIMIT = 56 * 2**20
+VMEM_LIMIT = 32 * 2**20
 MESH = pl.DeviceIdType.MESH
 
 
@@ -158,8 +160,6 @@
     peers = [partner(dim) for dim in range(bits)] + [(stn, *far(dz, dc)) for dz, dc in offsets[1:]]
     for peer in peers:
         pl.semaphore_signal(barrier, inc=1, device_id=peer, device_id_type=MESH)
-    pl.semaphore_wait(barrier, len(peers))
-
     def halo_copy(c):
         return pltpu.make_async_remote_copy(
             src_ref=own_ref.at[:, c, :, pl.ds(0, halo)],
@@ -169,15 +169,6 @@
             device_id=(stn, chan, core - 1),
             device_id_type=MESH,
         )
-
-    @pl.when(core > 0)
-    def _():
-        for c in range(chans):
-            halo_copy(c).start()
-
-    @pl.when(core == n_core - 1)
-    def _():
-        volts[:, :, :, samples:] = jnp.zeros((2, chans, stations, halo), volts.dtype)
 
     for copy in small:
         copy.wait()
@@ -193,6 +184,16 @@
             early = rolled[u - 1 : u] if u > 0 else jnp.zeros((1, fine), jnp.float32)
             row = jnp.where(column >= shift, late, early)
             wide_taps[phase, u] = jnp.broadcast_to(row, (16, fine)).astype(jnp.bfloat16)
+
+    pl.semaphore_wait(barrier, len(peers))
+
+    @pl.when(core > 0)
+    def _():
+        halo_copy(0).start()
+
+    @pl.when(core == n_core - 1)
+    def _():
+        volts[:, :, :, samples:] = jnp.zeros((2, chans, stations, halo), volts.dtype)
 
     def widened(value, count):
         wide_int[...] = jnp.zeros(wide_int.shape, jnp.int32)
@@ -295,8 +296,7 @@
             both = [v.reshape(n_stn, per, LANES) for v in (top, bottom)]
             return jnp.stack(both, axis=1).reshape(2 * beams, LANES)
 
-        @pl.loop(0, quads, unroll=BEAM_UNROLL)
-        def _(quad):
+        def one(quad):
             first = weight = (state[0], state[1])
             outs = []
             for q in range(QUAD):
@@ -340,6 +340,11 @@
                         d * rows : (d + 1) * rows
                     ]
 
+        for quad in range(quads):
+            one(quad)
+            if (quad + 1) % (quads // 2) == 0:
+                hop_copy(chunk, quad // (quads // 2), 0).start()
+
     def region(order, stage, last):
         index = [slice(None)] * bits
         for dim in orders[order][:stage]:
@@ -422,48 +427,50 @@
                 deliver(chunk, number).start()
             keep(chunk).start()
 
-    @pl.loop(0, chunks + bits)
-    def _(tick):
-        @pl.when(tick < chunks)
-        def _():
-            c = tick // halves
-            half = tick % halves
-
-            @pl.when(half == 0)
-            def _():
-                fetch(c).wait()
-
-                @pl.when(core < n_core - 1)
-                def _():
-                    halo_copy(c).wait_recv()
-
-                filter_channel(c)
-                transform()
-
-            form_beams(tick, c, half)
-            for order in range(2):
-                hop_copy(tick, order, 0).start()
-
-        for stage in range(1, bits + 1):
-            chunk = tick - stage
-
-            @pl.when((chunk >= 0) & (chunk < chunks))
-            def _(chunk=chunk, stage=stage):
-                step(chunk, stage)
-
-    @pl.when(core > 0)
-    def _():
-        for c in range(chans):
-            halo_copy(c).wait_send()
-
-    @pl.loop(0, chunks)
-    def _(chunk):
+    def drain(chunk):
         for order in range(2):
             for stage in range(bits):
                 hop_copy(chunk, order, stage).wait_send()
         for number in range(1, len(offsets)):
             deliver(chunk, number).wait()
         keep(chunk).wait()
+
+    @pl.loop(0, chunks + LEAD + bits + DELAY + DRAIN)
+    def _(tick):
+        def during(chunk, action):
+            @pl.when((chunk >= 0) & (chunk < chunks))
+            def _():
+                action(chunk)
+
+        during(tick - LEAD, lambda chunk: form_beams(chunk, chunk // halves, chunk % halves))
+        c = tick // halves
+
+        @pl.when((tick % halves == 0) & (c < chans))
+        def _():
+            fetch(c).wait()
+
+            @pl.when(core < n_core - 1)
+            def _():
+                halo_copy(c).wait_recv()
+
+            @pl.when((core > 0) & (c + 1 < chans))
+            def _():
+                halo_copy(c + 1).start()
+
+            filter_channel(c)
+
+        @pl.when((tick % halves == halves - 1) & (c < chans))
+        def _():
+            transform()
+
+        for stage in range(1, bits + 1):
+            during(tick - LEAD - DELAY - stage, lambda chunk, stage=stage: step(chunk, stage))
+        during(tick - LEAD - DELAY - bits - DRAIN, drain)
+
+    @pl.when(core > 0)
+    def _():
+        for c in range(chans):
+            halo_copy(c).wait_send()
 
 
 def body(volts, taps, delays, station_sub, beam_sub):
@@ -536,12 +543,17 @@
         ),
         name="channelize_and_beamform",
     )(
-        own,
-        taps,
-        dft_table(fine, lane_groups),
-        delays,
-        station_sub[None],
-        beam_sub[None],
+        *(
+            pltpu.with_memory_space_constraint(x, pltpu.HBM)
+            for x in (
+                own,
+                taps,
+                dft_table(fine, lane_groups),
+                delays,
+                station_sub[None],
+                beam_sub[None],
+            )
+        )
     )
     return out.reshape(per_device, 2, n_chan * chans, n_core * frames, fine).astype(jnp.float32)
 

time: 45.4 us -> 42.5 us (0.936)
  Pallas kernels: 43.1 us -> 41.1 us
  other arithmetic: 2.21 us -> 1.18 us
    pallas_call x1, Pallas kernels: 43.1 us -> 41.1 us  [body(): pl.pallas_call(functools.partial(kernel, (n_chan, n_core, bits), amplitud...]
    convert_element_type x1, other arithmetic: 2.21 us -> 1.18 us  [body(): out.reshape(per_device, 2, n_chan * chans, n_core * frames, fine)]
where the time goes in v3:
time: 42.5 us; the launch traced here: 42.2 us
  Pallas kernels  41.1 us (97%)
  other arithmetic  1.18 us (3%)
    pallas_call x1, Pallas kernels, body(): pl.pallas_call(functools.partial(kernel, (n_chan, n_core, bits), amplitud...  41.1 us
    convert_element_type x1, other arithmetic, body(): out.reshape(per_device, 2, n_chan * chans, n_core * frames, fine)  1.18 us

profile of v3, /device:TPU:0, one launch (start us, length us, event | category | flops | bytes accessed | tf_op | source)
XLA Modules:
  0.0 42.2 jit_solution(7248738969946811295)
XLA Ops:
  0.0 41.1 %channelize_and_beamform.1 = bf16[1,2,12,2,24,256]{5,4,3,2,1,0:T(8,128)(2,1)S(1)} custom-call(bf16[2,3,32,4608]{3,2,1,0:T(8,128)(2,1)} %bitcast.6, f32[16,256]{1,0:T(8,128)} %taps_hbm.1, bf16[512,512]{1,0:T(8,128)(2,1)} %constant.2.clone.table_hbm, s32[32,32]{1,0:T(8,128)} %delays_hbm.1, s32[1,32]{1,0:T(1,128)} %bitcast.7, s32[1,32]{1,0:T(1,128)} %bitcast.8), custom_call_target="tpu_custom_call" | custom-call | tf_op jit(solution)/shard_map/channelize_and_beamform/pallas_call | solution.py:504
  41.1 1.2 %bitcast_convert_fusion = f32[1,2,12,48,256]{4,3,2,1,0:T(8,128)} fusion(bf16[1,2,12,2,24,256]{5,4,3,2,1,0:T(8,128)(2,1)S(1)} %channelize_and_beamform.1), kind=kLoop, calls=%fused_computation | loop fusion | flops 294912 | bytes 1769472 | tf_op jit(solution)/shard_map/convert_element_type | solution.py:558

commit v4 on v3

--- a/solution.py
+++ b/solution.py
@@ -15,7 +15,7 @@
 WIDE = 2
 UNROLL_FB = True
 LEAD = 2
-DELAY = 0
+LATE = 1
 DRAIN = 3
 PHASES = 4
 VMEM_LIMIT = 32 * 2**20
@@ -33,7 +33,7 @@
     for half in range(fine // LANES):
         k = half * LANES + (np.arange(LANES).reshape(-1, lane_groups).T).reshape(-1)
         halves.append(np.concatenate([whole[0][:, k].T, whole[1][:, k].T]))
-    return jnp.asarray(np.concatenate(halves), jnp.bfloat16)
+    return jnp.asarray(np.stack(halves), jnp.bfloat16)
 
 
 def unit_turn(turn):
@@ -160,15 +160,19 @@
     peers = [partner(dim) for dim in range(bits)] + [(stn, *far(dz, dc)) for dz, dc in offsets[1:]]
     for peer in peers:
         pl.semaphore_signal(barrier, inc=1, device_id=peer, device_id_type=MESH)
-    def halo_copy(c):
+    def halo_copy(c, ri):
         return pltpu.make_async_remote_copy(
-            src_ref=own_ref.at[:, c, :, pl.ds(0, halo)],
-            dst_ref=volts.at[:, c, :, pl.ds(samples, halo)],
-            send_sem=halo_send.at[c],
-            recv_sem=halo_recv.at[c],
+            src_ref=own_ref.at[ri, c, :, pl.ds(0, halo)],
+            dst_ref=volts.at[ri, c, :, pl.ds(samples, halo)],
+            send_sem=halo_send.at[c, ri],
+            recv_sem=halo_recv.at[c, ri],
             device_id=(stn, chan, core - 1),
             device_id_type=MESH,
         )
+
+    def send_halo(c):
+        for ri in range(2):
+            halo_copy(c, ri).start()
 
     for copy in small:
         copy.wait()
@@ -189,7 +193,7 @@
 
     @pl.when(core > 0)
     def _():
-        halo_copy(0).start()
+        send_halo(0)
 
     @pl.when(core == n_core - 1)
     def _():
@@ -222,6 +226,14 @@
     def filter_channel(c):
         @pl.loop(0, 2)
         def _(ri):
+            @pl.when(core < n_core - 1)
+            def _():
+                halo_copy(c, ri).wait_recv()
+
+            @pl.when((core > 0) & (c + 1 < chans))
+            def _():
+                halo_copy(c + 1, ri).start()
+
             for half in range(halves):
                 for phase in range(PHASES):
                     shift = hop * phase % fine
@@ -249,27 +261,26 @@
                             pl.ds(pl.multiple_of(ri * fine + half * LANES, LANES), LANES),
                         ] = (sums[g][0] + sums[g][1]).reshape(stations, LANES)
 
-    def transform():
+    def transform(half):
         count = LANES // lane_groups
 
         def one(fb):
             rhs = filtered[pl.ds(pl.multiple_of(fb * LANES, LANES), WIDE * LANES), :]
             result = lax.dot_general(
-                table[...], rhs, (((1,), (1,)), ((), ())), preferred_element_type=jnp.float32
+                table[half], rhs, (((1,), (1,)), ((), ())), preferred_element_type=jnp.float32
             )
-            for half in range(halves):
-                for ri in range(2):
-                    for sub in range(WIDE):
-                        pieces = [
-                            result[
-                                ((half * 2 + ri) * lane_groups + j) * count : ((half * 2 + ri) * lane_groups + j + 1) * count,
-                                sub * LANES : (sub + 1) * LANES,
-                            ]
-                            for j in range(lane_groups)
+            for ri in range(2):
+                for sub in range(WIDE):
+                    pieces = [
+                        result[
+                            (ri * lane_groups + j) * count : (ri * lane_groups + j + 1) * count,
+                            sub * LANES : (sub + 1) * LANES,
                         ]
-                        for j, piece in enumerate(swap_index_with_lanes(pieces, stations)):
-                            at = pl.multiple_of(((fb + sub) * lane_groups + j) * count, count)
-                            spectra[half, ri, pl.ds(at, count), :] = piece
+                        for j in range(lane_groups)
+                    ]
+                    for j, piece in enumerate(swap_index_with_lanes(pieces, stations)):
+                        at = pl.multiple_of(((fb + sub) * lane_groups + j) * count, count)
+                        spectra[half, ri, pl.ds(at, count), :] = piece
 
         if UNROLL_FB:
             for fb in range(0, frames // lane_groups, WIDE):
@@ -435,7 +446,7 @@
             deliver(chunk, number).wait()
         keep(chunk).wait()
 
-    @pl.loop(0, chunks + LEAD + bits + DELAY + DRAIN)
+    @pl.loop(0, chunks + LEAD + bits + LATE + DRAIN)
     def _(tick):
         def during(chunk, action):
             @pl.when((chunk >= 0) & (chunk < chunks))
@@ -445,32 +456,25 @@
         during(tick - LEAD, lambda chunk: form_beams(chunk, chunk // halves, chunk % halves))
         c = tick // halves
 
+        @pl.when((tick >= 1) & (tick <= chunks))
+        def _():
+            transform((tick - 1) % halves)
+
         @pl.when((tick % halves == 0) & (c < chans))
         def _():
             fetch(c).wait()
-
-            @pl.when(core < n_core - 1)
-            def _():
-                halo_copy(c).wait_recv()
-
-            @pl.when((core > 0) & (c + 1 < chans))
-            def _():
-                halo_copy(c + 1).start()
-
             filter_channel(c)
 
-        @pl.when((tick % halves == halves - 1) & (c < chans))
-        def _():
-            transform()
-
         for stage in range(1, bits + 1):
-            during(tick - LEAD - DELAY - stage, lambda chunk, stage=stage: step(chunk, stage))
-        during(tick - LEAD - DELAY - bits - DRAIN, drain)
+            behind = stage + (LATE if stage == bits else 0)
+            during(tick - LEAD - behind, lambda chunk, stage=stage: step(chunk, stage))
+        during(tick - LEAD - LATE - bits - DRAIN, drain)
 
     @pl.when(core > 0)
     def _():
         for c in range(chans):
-            halo_copy(c).wait_send()
+            for ri in range(2):
+                halo_copy(c, ri).wait_send()
 
 
 def body(volts, taps, delays, station_sub, beam_sub):
@@ -511,7 +515,7 @@
         scratch_shapes=[
             pltpu.VMEM((2, chans, stations, blocks * fine), jnp.bfloat16),
             pltpu.VMEM((tap_count, fine), jnp.float32),
-            pltpu.VMEM((halves * 2 * LANES, 2 * fine), jnp.bfloat16),
+            pltpu.VMEM((halves, 2 * LANES, 2 * fine), jnp.bfloat16),
             pltpu.VMEM((beams, stations), jnp.int32),
             pltpu.VMEM((1, stations), jnp.int32),
             pltpu.VMEM((1, beams), jnp.int32),
@@ -528,8 +532,8 @@
             pltpu.VMEM((chunks, n_chan, n_core, per_device, 2, frames, LANES), jnp.bfloat16),
             dma((chans,)),
             dma((5,)),
-            dma((chans,)),
-            dma((chans,)),
+            dma((chans, 2)),
+            dma((chans, 2)),
             dma((bits, chunks, 2)),
             dma((bits, chunks, 2)),
             dma((chunks, peers)),

time: 42.5 us -> 41 us (0.965)
  Pallas kernels: 41.1 us -> 39.5 us
    pallas_call x1, Pallas kernels: 41.1 us -> 39.5 us  [body(): pl.pallas_call(functools.partial(kernel, (n_chan, n_core, bits), amplitud...]
where the time goes in v4:
time: 41 us; the launch traced here: 40.7 us
  Pallas kernels  39.5 us (96%)
  other arithmetic  1.18 us (3%)
    pallas_call x1, Pallas kernels, body(): pl.pallas_call(functools.partial(kernel, (n_chan, n_core, bits), amplitud...  39.5 us
    convert_element_type x1, other arithmetic, body(): out.reshape(per_device, 2, n_chan * chans, n_core * frames, fine)  1.18 us

profile of v4, /device:TPU:0, one launch (start us, length us, event | category | flops | bytes accessed | tf_op | source)
XLA Modules:
  0.0 40.7 jit_solution(802583774748196081)
XLA Ops:
  0.0 39.5 %channelize_and_beamform.1 = bf16[1,2,12,2,24,256]{5,4,3,2,1,0:T(8,128)(2,1)S(1)} custom-call(bf16[2,3,32,4608]{3,2,1,0:T(8,128)(2,1)} %bitcast.6, f32[16,256]{1,0:T(8,128)} %taps_hbm.1, bf16[2,256,512]{2,1,0:T(8,128)(2,1)} %constant.2.clone.table_hbm, s32[32,32]{1,0:T(8,128)} %delays_hbm.1, s32[1,32]{1,0:T(1,128)} %bitcast.7, s32[1,32]{1,0:T(1,128)} %bitcast.8), custom_call_target="tpu_custom_call" | custom-call | tf_op jit(solution)/shard_map/channelize_and_beamform/pallas_call | solution.py:508
  39.5 1.2 %bitcast_convert_fusion = f32[1,2,12,48,256]{4,3,2,1,0:T(8,128)} fusion(bf16[1,2,12,2,24,256]{5,4,3,2,1,0:T(8,128)(2,1)S(1)} %channelize_and_beamform.1), kind=kLoop, calls=%fused_computation | loop fusion | flops 294912 | bytes 1769472 | tf_op jit(solution)/shard_map/convert_element_type | solution.py:562

commit v5 on v4

--- a/solution.py
+++ b/solution.py
@@ -16,7 +16,7 @@
 UNROLL_FB = True
 LEAD = 2
 LATE = 1
-DRAIN = 3
+PIECES = 2
 PHASES = 4
 VMEM_LIMIT = 32 * 2**20
 MESH = pl.DeviceIdType.MESH
@@ -101,7 +101,6 @@
     recv,
     far_send,
     far_recv,
-    keep_sem,
     *exchanged,
 ):
     n_chan, n_core, bits = sizes
@@ -347,21 +346,21 @@
                 value = value.astype(jnp.bfloat16)
                 for d in range(n_stn):
                     place = [(d >> (bits - 1 - dim)) & 1 for dim in range(bits)]
-                    part[(chunk, quad // (quads // 2), *place, quad % (quads // 2), t)] = value[
+                    part[(chunk, quad // (quads // PIECES), *place, quad % (quads // PIECES), t)] = value[
                         d * rows : (d + 1) * rows
                     ]
 
         for quad in range(quads):
             one(quad)
-            if (quad + 1) % (quads // 2) == 0:
-                hop_copy(chunk, quad // (quads // 2), 0).start()
+            if (quad + 1) % (quads // PIECES) == 0:
+                hop_copy(chunk, quad // (quads // PIECES), 0).start()
 
     def region(order, stage, last):
         index = [slice(None)] * bits
-        for dim in orders[order][:stage]:
+        for dim in orders[order % 2][:stage]:
             index[dim] = own_bit[dim]
         if stage < bits:
-            index[orders[order][stage]] = last(orders[order][stage])
+            index[orders[order % 2][stage]] = last(orders[order % 2][stage])
         return index
 
     def other(dim):
@@ -370,7 +369,7 @@
     def with_received(chunk, order, stage, index):
         value = part[(chunk, order, *index)].astype(jnp.float32)
         for earlier in range(stage):
-            kept = [dim for dim in range(bits) if dim not in orders[order][: earlier + 1]]
+            kept = [dim for dim in range(bits) if dim not in orders[order % 2][: earlier + 1]]
             piece = received[earlier][(chunk, order, *(index[dim] for dim in kept))]
             value = value + piece.astype(jnp.float32)
         return value
@@ -383,9 +382,9 @@
         return pltpu.make_async_remote_copy(
             src_ref=source,
             dst_ref=received[stage].at[chunk, order],
-            send_sem=send.at[stage, chunk, order],
+            send_sem=send.at[stage],
             recv_sem=recv.at[stage, chunk, order],
-            device_id=partner(orders[order][stage]),
+            device_id=partner(orders[order % 2][stage]),
             device_id_type=MESH,
         )
 
@@ -399,20 +398,20 @@
         return pltpu.make_async_remote_copy(
             src_ref=final.at[chunk, z, k],
             dst_ref=place_of(chunk),
-            send_sem=far_send.at[chunk, number],
-            recv_sem=far_recv.at[chunk, number],
+            send_sem=far_send,
+            recv_sem=far_recv,
             device_id=(stn, z, k),
             device_id_type=MESH,
         )
 
     def keep(chunk):
-        return pltpu.make_async_copy(final.at[chunk, chan, core], place_of(chunk), keep_sem.at[chunk])
+        return pltpu.make_async_copy(final.at[chunk, chan, core], place_of(chunk), far_recv)
 
     def finish(chunk):
-        for order in range(2):
+        for order in range(PIECES):
             value = with_received(chunk, order, bits, own_bit)
-            for quad in range(quads // 2):
-                at = (order * (quads // 2) + quad) * rows
+            for quad in range(quads // PIECES):
+                at = (order * (quads // PIECES) + quad) * rows
                 for t in range(tiles):
                     total_ref[t, at : at + rows, :] = value[quad, t]
         for t in range(tiles):
@@ -425,7 +424,7 @@
             final[chunk, z, k, at, ri] = piece.astype(jnp.bfloat16)
 
     def step(chunk, stage):
-        for order in range(2):
+        for order in range(PIECES):
             hop_copy(chunk, order, stage - 1).wait_recv()
             if stage < bits:
                 sent[stage - 1][chunk, order] = with_received(
@@ -438,15 +437,7 @@
                 deliver(chunk, number).start()
             keep(chunk).start()
 
-    def drain(chunk):
-        for order in range(2):
-            for stage in range(bits):
-                hop_copy(chunk, order, stage).wait_send()
-        for number in range(1, len(offsets)):
-            deliver(chunk, number).wait()
-        keep(chunk).wait()
-
-    @pl.loop(0, chunks + LEAD + bits + LATE + DRAIN)
+    @pl.loop(0, chunks + LEAD + bits)
     def _(tick):
         def during(chunk, action):
             @pl.when((chunk >= 0) & (chunk < chunks))
@@ -465,16 +456,41 @@
             fetch(c).wait()
             filter_channel(c)
 
-        for stage in range(1, bits + 1):
-            behind = stage + (LATE if stage == bits else 0)
-            during(tick - LEAD - behind, lambda chunk, stage=stage: step(chunk, stage))
-        during(tick - LEAD - LATE - bits - DRAIN, drain)
+        for stage in range(1, bits):
+            during(tick - LEAD - stage, lambda chunk, stage=stage: step(chunk, stage))
+
+        def summed(tick):
+            caught_up = jnp.where(tick >= LEAD + chunks - 1, LATE, 0)
+            return jnp.clip(tick - LEAD - bits - LATE + 1 + caught_up, 0, chunks)
+
+        @pl.loop(summed(tick - 1), summed(tick))
+        def _(chunk):
+            step(chunk, bits)
+
 
     @pl.when(core > 0)
     def _():
         for c in range(chans):
             for ri in range(2):
                 halo_copy(c, ri).wait_send()
+
+    def all_of(ref, send_sem, recv_sem):
+        return pltpu.make_async_remote_copy(
+            src_ref=ref,
+            dst_ref=ref,
+            send_sem=send_sem,
+            recv_sem=recv_sem,
+            device_id=partner(0),
+            device_id_type=MESH,
+        )
+
+    for stage in range(bits):
+        all_of(received[stage], send.at[stage], far_recv).wait_send()
+    if n_chan > 1:
+        all_of(final.at[:, 0 : n_chan - 1], far_send, far_recv).wait_send()
+    if n_core > 1:
+        all_of(final.at[:, 0, 0 : n_core - 1], far_send, far_recv).wait_send()
+    all_of(out_ref, far_send, far_recv).wait_recv()
 
 
 def body(volts, taps, delays, station_sub, beam_sub):
@@ -494,14 +510,13 @@
     quads = LANES // lane_groups // QUAD
     tiles = QUAD * frames * lane_groups // LANES
     rows = 2 * per
-    peers = n_chan * n_core
     assert n_stn == 2**bits and rows == QUAD * lane_groups and quads * rows == LANES
     assert QUAD * frames * lane_groups == tiles * LANES and frames * lane_groups <= LANES
     blocks = hop * (PHASES - 1) // fine + tap_count + 1 + 3 * (frames // PHASES - 1)
     amplitude = 1.0 / math.sqrt(stations * n_stn // SUBARRAYS)
-    block = (quads // 2, tiles, rows, LANES)
+    block = (quads // PIECES, tiles, rows, LANES)
     pieces = [
-        pltpu.VMEM((chunks, 2) + (2,) * (bits - 1 - t) + block, jnp.bfloat16) for t in range(bits)
+        pltpu.VMEM((chunks, PIECES) + (2,) * (bits - 1 - t) + block, jnp.bfloat16) for t in range(bits)
     ]
     hbm = pl.BlockSpec(memory_space=pltpu.HBM)
     dma = pltpu.SemaphoreType.DMA
@@ -528,17 +543,16 @@
             pltpu.VMEM((halves, 2, frames * LANES // lane_groups, LANES), jnp.float32),
             pltpu.VMEM((tiles, LANES, LANES), jnp.float32),
             pltpu.VMEM((tiles * LANES, LANES), jnp.float32),
-            pltpu.VMEM((chunks, 2) + (2,) * bits + block, jnp.bfloat16),
+            pltpu.VMEM((chunks, PIECES) + (2,) * bits + block, jnp.bfloat16),
             pltpu.VMEM((chunks, n_chan, n_core, per_device, 2, frames, LANES), jnp.bfloat16),
             dma((chans,)),
             dma((5,)),
             dma((chans, 2)),
             dma((chans, 2)),
-            dma((bits, chunks, 2)),
-            dma((bits, chunks, 2)),
-            dma((chunks, peers)),
-            dma((chunks, peers)),
-            dma((chunks,)),
+            dma((bits,)),
+            dma((bits, chunks, PIECES)),
+            dma,
+            dma,
             *pieces,
             *pieces[1:],
         ],

time: 41 us -> 39.8 us (0.971)
  Pallas kernels: 39.5 us -> 38.4 us
    pallas_call x1, Pallas kernels: 39.5 us -> 38.4 us  [body(): pl.pallas_call(functools.partial(kernel, (n_chan, n_core, bits), amplitud...]
where the time goes in v5:
time: 39.8 us; the launch traced here: 39.6 us
  Pallas kernels  38.4 us (96%)
  other arithmetic  1.18 us (3%)
    pallas_call x1, Pallas kernels, body(): pl.pallas_call(functools.partial(kernel, (n_chan, n_core, bits), amplitud...  38.4 us
    convert_element_type x1, other arithmetic, body(): out.reshape(per_device, 2, n_chan * chans, n_core * frames, fine)  1.18 us

profile of v5, /device:TPU:0, one launch (start us, length us, event | category | flops | bytes accessed | tf_op | source)
XLA Modules:
  0.0 39.6 jit_solution(13898995341727186621)
XLA Ops:
  0.0 38.4 %channelize_and_beamform.1 = bf16[1,2,12,2,24,256]{5,4,3,2,1,0:T(8,128)(2,1)S(1)} custom-call(bf16[2,3,32,4608]{3,2,1,0:T(8,128)(2,1)} %bitcast.6, f32[16,256]{1,0:T(8,128)} %taps_hbm.1, bf16[2,256,512]{2,1,0:T(8,128)(2,1)} %constant.2.clone.table_hbm, s32[32,32]{1,0:T(8,128)} %delays_hbm.1, s32[1,32]{1,0:T(1,128)} %bitcast.7, s32[1,32]{1,0:T(1,128)} %bitcast.8), custom_call_target="tpu_custom_call" | custom-call | tf_op jit(solution)/shard_map/channelize_and_beamform/pallas_call | solution.py:523
  38.4 1.2 %bitcast_convert_fusion = f32[1,2,12,48,256]{4,3,2,1,0:T(8,128)} fusion(bf16[1,2,12,2,24,256]{5,4,3,2,1,0:T(8,128)(2,1)S(1)} %channelize_and_beamform.1), kind=kLoop, calls=%fused_computation | loop fusion | flops 294912 | bytes 1769472 | tf_op jit(solution)/shard_map/convert_element_type | solution.py:576

commit v6 on v5

--- a/solution.py
+++ b/solution.py
@@ -140,11 +140,6 @@
             )
         )
     ]
-    for copy in small:
-        copy.start()
-    for c in range(chans):
-        fetch(c).start()
-
     own_bit = [(stn // 2 ** (bits - 1 - dim)) % 2 for dim in range(bits)]
     orders = (tuple(range(bits - 1, -1, -1)), tuple(range(bits)))
 
@@ -159,6 +154,13 @@
     peers = [partner(dim) for dim in range(bits)] + [(stn, *far(dz, dc)) for dz, dc in offsets[1:]]
     for peer in peers:
         pl.semaphore_signal(barrier, inc=1, device_id=peer, device_id_type=MESH)
+    small[0].start()
+    fetch(0).start()
+    for copy in small[1:]:
+        copy.start()
+    for c in range(1, chans):
+        fetch(c).start()
+
     def halo_copy(c, ri):
         return pltpu.make_async_remote_copy(
             src_ref=own_ref.at[ri, c, :, pl.ds(0, halo)],
@@ -173,8 +175,17 @@
         for ri in range(2):
             halo_copy(c, ri).start()
 
-    for copy in small:
-        copy.wait()
+    small[0].wait()
+
+    pl.semaphore_wait(barrier, len(peers))
+
+    @pl.when(core > 0)
+    def _():
+        send_halo(0)
+
+    @pl.when(core == n_core - 1)
+    def _():
+        volts[:, :, :, samples:] = jnp.zeros((2, chans, stations, halo), volts.dtype)
 
     for phase in range(PHASES):
         shift = hop * phase % fine
@@ -188,15 +199,8 @@
             row = jnp.where(column >= shift, late, early)
             wide_taps[phase, u] = jnp.broadcast_to(row, (16, fine)).astype(jnp.bfloat16)
 
-    pl.semaphore_wait(barrier, len(peers))
-
-    @pl.when(core > 0)
-    def _():
-        send_halo(0)
-
-    @pl.when(core == n_core - 1)
-    def _():
-        volts[:, :, :, samples:] = jnp.zeros((2, chans, stations, halo), volts.dtype)
+    for copy in small[1:]:
+        copy.wait()
 
     def widened(value, count):
         wide_int[...] = jnp.zeros(wide_int.shape, jnp.int32)
@@ -222,9 +226,13 @@
         steps[i, 0] = c
         steps[i, 1] = -s
 
-    def filter_channel(c):
-        @pl.loop(0, 2)
+    def filter_channel(c, first_part, last_part):
+        @pl.loop(first_part, last_part)
         def _(ri):
+            @pl.when(ri == 0)
+            def _():
+                fetch(c).wait()
+
             @pl.when(core < n_core - 1)
             def _():
                 halo_copy(c, ri).wait_recv()
@@ -256,15 +264,18 @@
                     for g in range(groups):
                         f = PHASES * g + phase
                         filtered[
+                            c % 2,
                             f * stations : (f + 1) * stations,
                             pl.ds(pl.multiple_of(ri * fine + half * LANES, LANES), LANES),
                         ] = (sums[g][0] + sums[g][1]).reshape(stations, LANES)
 
-    def transform(half):
+    def transform(chunk):
+        half = chunk % halves
+        slot = chunk // halves % 2
         count = LANES // lane_groups
 
         def one(fb):
-            rhs = filtered[pl.ds(pl.multiple_of(fb * LANES, LANES), WIDE * LANES), :]
+            rhs = filtered[slot, pl.ds(pl.multiple_of(fb * LANES, LANES), WIDE * LANES), :]
             result = lax.dot_general(
                 table[half], rhs, (((1,), (1,)), ((), ())), preferred_element_type=jnp.float32
             )
@@ -447,14 +458,13 @@
         during(tick - LEAD, lambda chunk: form_beams(chunk, chunk // halves, chunk % halves))
         c = tick // halves
 
+        @pl.when((c < chans) & (tick != 1))
+        def _():
+            filter_channel(c, tick % 2, jnp.where(tick == 0, 2, tick % 2 + 1))
+
         @pl.when((tick >= 1) & (tick <= chunks))
         def _():
-            transform((tick - 1) % halves)
-
-        @pl.when((tick % halves == 0) & (c < chans))
-        def _():
-            fetch(c).wait()
-            filter_channel(c)
+            transform(tick - 1)
 
         for stage in range(1, bits):
             during(tick - LEAD - stage, lambda chunk, stage=stage: step(chunk, stage))
@@ -510,7 +520,7 @@
     quads = LANES // lane_groups // QUAD
     tiles = QUAD * frames * lane_groups // LANES
     rows = 2 * per
-    assert n_stn == 2**bits and rows == QUAD * lane_groups and quads * rows == LANES
+    assert halves == 2 and n_stn == 2**bits and rows == QUAD * lane_groups and quads * rows == LANES
     assert QUAD * frames * lane_groups == tiles * LANES and frames * lane_groups <= LANES
     blocks = hop * (PHASES - 1) // fine + tap_count + 1 + 3 * (frames // PHASES - 1)
     amplitude = 1.0 / math.sqrt(stations * n_stn // SUBARRAYS)
@@ -539,7 +549,7 @@
             pltpu.VMEM((beams, LANES), jnp.float32),
             pltpu.VMEM((2, 2, beams, LANES), jnp.float32),
             pltpu.VMEM((2, beams, LANES), jnp.float32),
-            pltpu.VMEM((frames * stations, 2 * fine), jnp.bfloat16),
+            pltpu.VMEM((2, frames * stations, 2 * fine), jnp.bfloat16),
             pltpu.VMEM((halves, 2, frames * LANES // lane_groups, LANES), jnp.float32),
             pltpu.VMEM((tiles, LANES, LANES), jnp.float32),
             pltpu.VMEM((tiles * LANES, LANES), jnp.float32),

time: 39.8 us -> 39.2 us (0.985)
  Pallas kernels: 38.4 us -> 37.8 us
    pallas_call x1, Pallas kernels: 38.4 us -> 37.8 us  [body(): pl.pallas_call(functools.partial(kernel, (n_chan, n_core, bits), amplitud...]
where the time goes in v6:
time: 39.2 us; the launch traced here: 39 us
  Pallas kernels  37.8 us (96%)
  other arithmetic  1.18 us (3%)
    pallas_call x1, Pallas kernels, body(): pl.pallas_call(functools.partial(kernel, (n_chan, n_core, bits), amplitud...  37.8 us
    convert_element_type x1, other arithmetic, body(): out.reshape(per_device, 2, n_chan * chans, n_core * frames, fine)  1.18 us

profile of v6, /device:TPU:0, one launch (start us, length us, event | category | flops | bytes accessed | tf_op | source)
XLA Modules:
  0.0 39.0 jit_solution(7419360845767120247)
XLA Ops:
  0.0 37.8 %channelize_and_beamform.1 = bf16[1,2,12,2,24,256]{5,4,3,2,1,0:T(8,128)(2,1)S(1)} custom-call(bf16[2,3,32,4608]{3,2,1,0:T(8,128)(2,1)} %bitcast.6, f32[16,256]{1,0:T(8,128)} %taps_hbm.1, bf16[2,256,512]{2,1,0:T(8,128)(2,1)} %constant.2.clone.table_hbm, s32[32,32]{1,0:T(8,128)} %delays_hbm.1, s32[1,32]{1,0:T(1,128)} %bitcast.7, s32[1,32]{1,0:T(1,128)} %bitcast.8), custom_call_target="tpu_custom_call" | custom-call | tf_op jit(solution)/shard_map/channelize_and_beamform/pallas_call | solution.py:533
  37.8 1.2 %bitcast_convert_fusion = f32[1,2,12,48,256]{4,3,2,1,0:T(8,128)} fusion(bf16[1,2,12,2,24,256]{5,4,3,2,1,0:T(8,128)(2,1)S(1)} %channelize_and_beamform.1), kind=kLoop, calls=%fused_computation | loop fusion | flops 294912 | bytes 1769472 | tf_op jit(solution)/shard_map/convert_element_type | solution.py:586

commit v7 on v6

--- a/solution.py
+++ b/solution.py
@@ -226,6 +226,49 @@
         steps[i, 0] = c
         steps[i, 1] = -s
 
+    def filter_part(c, ri, local):
+        limit = samples // fine
+        for half in range(halves):
+            for phase in range(PHASES):
+                shift = hop * phase % fine
+                block0 = hop * phase // fine
+                first = 0 if shift < (half + 1) * LANES else 1
+                last = tap_count - 1 if shift <= half * LANES else tap_count
+                lanes = slice(half * LANES, (half + 1) * LANES)
+                taps = {u: wide_taps[phase, u, :, lanes][None] for u in range(first, last + 1)}
+                columns = pl.ds(pl.multiple_of(ri * fine + half * LANES, LANES), LANES)
+                blocks = [
+                    block
+                    for block in range(block0 + first, block0 + last + 1 + 3 * (groups - 1))
+                    if (block < limit) == local
+                ]
+                for_group = [
+                    [block for block in blocks if first <= block - block0 - 3 * g <= last]
+                    for g in range(groups)
+                ]
+                sums = [[None, None] for _ in range(groups)]
+                for g in range(groups):
+                    f = PHASES * g + phase
+                    if not local and for_group[g] and block0 + 3 * g + first < limit:
+                        begun = filtered[c % 2, f * stations : (f + 1) * stations, columns]
+                        sums[g][0] = begun.reshape(stations // 16, 16, LANES)
+                for block in blocks:
+                    at = block * fine + half * LANES
+                    value = volts[ri, c, :, at : at + LANES].reshape(stations // 16, 16, LANES)
+                    for g in range(groups):
+                        if block in for_group[g]:
+                            u = block - block0 - 3 * g
+                            term = taps[u] * value
+                            so_far = sums[g][u % 2]
+                            sums[g][u % 2] = term if so_far is None else so_far + term
+                for g in range(groups):
+                    if for_group[g]:
+                        f = PHASES * g + phase
+                        parts = [part_sum for part_sum in sums[g] if part_sum is not None]
+                        filtered[c % 2, f * stations : (f + 1) * stations, columns] = sum(
+                            parts[1:], parts[0]
+                        ).reshape(stations, LANES)
+
     def filter_channel(c, first_part, last_part):
         @pl.loop(first_part, last_part)
         def _(ri):
@@ -233,6 +276,10 @@
             def _():
                 fetch(c).wait()
 
+            filter_part(c, ri, True)
+
+        @pl.loop(first_part, last_part)
+        def _(ri):
             @pl.when(core < n_core - 1)
             def _():
                 halo_copy(c, ri).wait_recv()
@@ -241,33 +288,7 @@
             def _():
                 halo_copy(c + 1, ri).start()
 
-            for half in range(halves):
-                for phase in range(PHASES):
-                    shift = hop * phase % fine
-                    block0 = hop * phase // fine
-                    first = 0 if shift < (half + 1) * LANES else 1
-                    last = tap_count - 1 if shift <= half * LANES else tap_count
-                    lanes = slice(half * LANES, (half + 1) * LANES)
-                    taps = {
-                        u: wide_taps[phase, u, :, lanes][None] for u in range(first, last + 1)
-                    }
-                    sums = [[None, None] for _ in range(groups)]
-                    for block in range(block0 + first, block0 + last + 1 + 3 * (groups - 1)):
-                        at = block * fine + half * LANES
-                        value = volts[ri, c, :, at : at + LANES].reshape(stations // 16, 16, LANES)
-                        for g in range(groups):
-                            u = block - block0 - 3 * g
-                            if first <= u <= last:
-                                term = taps[u] * value
-                                so_far = sums[g][u % 2]
-                                sums[g][u % 2] = term if so_far is None else so_far + term
-                    for g in range(groups):
-                        f = PHASES * g + phase
-                        filtered[
-                            c % 2,
-                            f * stations : (f + 1) * stations,
-                            pl.ds(pl.multiple_of(ri * fine + half * LANES, LANES), LANES),
-                        ] = (sums[g][0] + sums[g][1]).reshape(stations, LANES)
+            filter_part(c, ri, False)
 
     def transform(chunk):
         half = chunk % halves

time: 39.2 us -> 38.7 us (0.987)
  Pallas kernels: 37.8 us -> 37.3 us
    pallas_call x1, Pallas kernels: 37.8 us -> 37.3 us  [body(): pl.pallas_call(functools.partial(kernel, (n_chan, n_core, bits), amplitud...]
where the time goes in v7:
time: 38.7 us; the launch traced here: 38.4 us
  Pallas kernels  37.3 us (96%)
  other arithmetic  1.18 us (3%)
    pallas_call x1, Pallas kernels, body(): pl.pallas_call(functools.partial(kernel, (n_chan, n_core, bits), amplitud...  37.3 us
    convert_element_type x1, other arithmetic, body(): out.reshape(per_device, 2, n_chan * chans, n_core * frames, fine)  1.18 us

profile of v7, /device:TPU:0, one launch (start us, length us, event | category | flops | bytes accessed | tf_op | source)
XLA Modules:
  0.0 38.4 jit_solution(10959894609780975904)
XLA Ops:
  0.0 37.3 %channelize_and_beamform.1 = bf16[1,2,12,2,24,256]{5,4,3,2,1,0:T(8,128)(2,1)S(1)} custom-call(bf16[2,3,32,4608]{3,2,1,0:T(8,128)(2,1)} %bitcast.6, f32[16,256]{1,0:T(8,128)} %taps_hbm.1, bf16[2,256,512]{2,1,0:T(8,128)(2,1)} %constant.2.clone.table_hbm, s32[32,32]{1,0:T(8,128)} %delays_hbm.1, s32[1,32]{1,0:T(1,128)} %bitcast.7, s32[1,32]{1,0:T(1,128)} %bitcast.8), custom_call_target="tpu_custom_call" | custom-call | tf_op jit(solution)/shard_map/channelize_and_beamform/pallas_call | solution.py:554
  37.3 1.2 %bitcast_convert_fusion = f32[1,2,12,48,256]{4,3,2,1,0:T(8,128)} fusion(bf16[1,2,12,2,24,256]{5,4,3,2,1,0:T(8,128)(2,1)S(1)} %channelize_and_beamform.1), kind=kLoop, calls=%fused_computation | loop fusion | flops 294912 | bytes 1769472 | tf_op jit(solution)/shard_map/convert_element_type | solution.py:607

commit v8 on v7

--- a/solution.py
+++ b/solution.py
@@ -465,7 +465,7 @@
                 hop_copy(chunk, order, stage).start()
         if stage == bits:
             finish(chunk)
-            for number in range(len(offsets) - 1, 0, -1):
+            for number in range(1, len(offsets)):
                 deliver(chunk, number).start()
             keep(chunk).start()
 

time: 38.7 us -> 38.1 us (0.984)
  Pallas kernels: 37.3 us -> 36.7 us
    pallas_call x1, Pallas kernels: 37.3 us -> 36.7 us  [body(): pl.pallas_call(functools.partial(kernel, (n_chan, n_core, bits), amplitud...]
where the time goes in v8:
time: 38.1 us; the launch traced here: 37.9 us
  Pallas kernels  36.7 us (96%)
  other arithmetic  1.18 us (3%)
    pallas_call x1, Pallas kernels, body(): pl.pallas_call(functools.partial(kernel, (n_chan, n_core, bits), amplitud...  36.7 us
    convert_element_type x1, other arithmetic, body(): out.reshape(per_device, 2, n_chan * chans, n_core * frames, fine)  1.18 us

profile of v8, /device:TPU:0, one launch (start us, length us, event | category | flops | bytes accessed | tf_op | source)
XLA Modules:
  0.0 37.9 jit_solution(9560345089852336103)
XLA Ops:
  0.0 36.7 %channelize_and_beamform.1 = bf16[1,2,12,2,24,256]{5,4,3,2,1,0:T(8,128)(2,1)S(1)} custom-call(bf16[2,3,32,4608]{3,2,1,0:T(8,128)(2,1)} %bitcast.6, f32[16,256]{1,0:T(8,128)} %taps_hbm.1, bf16[2,256,512]{2,1,0:T(8,128)(2,1)} %constant.2.clone.table_hbm, s32[32,32]{1,0:T(8,128)} %delays_hbm.1, s32[1,32]{1,0:T(1,128)} %bitcast.7, s32[1,32]{1,0:T(1,128)} %bitcast.8), custom_call_target="tpu_custom_call" | custom-call | tf_op jit(solution)/shard_map/channelize_and_beamform/pallas_call | solution.py:554
  36.7 1.2 %bitcast_convert_fusion = f32[1,2,12,48,256]{4,3,2,1,0:T(8,128)} fusion(bf16[1,2,12,2,24,256]{5,4,3,2,1,0:T(8,128)(2,1)S(1)} %channelize_and_beamform.1), kind=kLoop, calls=%fused_computation | loop fusion | flops 294912 | bytes 1769472 | tf_op jit(solution)/shard_map/convert_element_type | solution.py:607

commit v9 on v8

--- a/solution.py
+++ b/solution.py
@@ -149,7 +149,7 @@
     def far(dz, dc):
         return ((chan + dz) % n_chan, (core + dc) % n_core)
 
-    offsets = [(dz, dc) for dz in range(n_chan) for dc in range(n_core)]
+    offsets = [(dz, dc) for dc in range(n_core) for dz in range(n_chan)]
     barrier = pltpu.get_barrier_semaphore()
     peers = [partner(dim) for dim in range(bits)] + [(stn, *far(dz, dc)) for dz, dc in offsets[1:]]
     for peer in peers:

time: 38.1 us -> 38.1 us (level)
  no operation moved by 1% of the time
where the time goes in v9:
time: 38.1 us; the launch traced here: 37.9 us
  Pallas kernels  36.7 us (96%)
  other arithmetic  1.18 us (3%)
    pallas_call x1, Pallas kernels, body(): pl.pallas_call(functools.partial(kernel, (n_chan, n_core, bits), amplitud...  36.7 us
    convert_element_type x1, other arithmetic, body(): out.reshape(per_device, 2, n_chan * chans, n_core * frames, fine)  1.18 us

profile of v9, /device:TPU:0, one launch (start us, length us, event | category | flops | bytes accessed | tf_op | source)
XLA Modules:
  0.0 37.9 jit_solution(3561334563437271474)
XLA Ops:
  0.0 36.7 %channelize_and_beamform.1 = bf16[1,2,12,2,24,256]{5,4,3,2,1,0:T(8,128)(2,1)S(1)} custom-call(bf16[2,3,32,4608]{3,2,1,0:T(8,128)(2,1)} %bitcast.6, f32[16,256]{1,0:T(8,128)} %taps_hbm.1, bf16[2,256,512]{2,1,0:T(8,128)(2,1)} %constant.2.clone.table_hbm, s32[32,32]{1,0:T(8,128)} %delays_hbm.1, s32[1,32]{1,0:T(1,128)} %bitcast.7, s32[1,32]{1,0:T(1,128)} %bitcast.8), custom_call_target="tpu_custom_call" | custom-call | tf_op jit(solution)/shard_map/channelize_and_beamform/pallas_call | solution.py:554
  36.7 1.2 %bitcast_convert_fusion = f32[1,2,12,48,256]{4,3,2,1,0:T(8,128)} fusion(bf16[1,2,12,2,24,256]{5,4,3,2,1,0:T(8,128)(2,1)S(1)} %channelize_and_beamform.1), kind=kLoop, calls=%fused_computation | loop fusion | flops 294912 | bytes 1769472 | tf_op jit(solution)/shard_map/convert_element_type | solution.py:607
